TPU v7x, 32 devices: a whole 2x2x4 slice. The times are simulated.
32 devices in a mesh: depth: 2 (over core), rows: 2 (over x), shots: 8 (over z, y).
Axes of the slice: x: 2, y: 2, z: 4, core: 2. Of those that a mesh axis runs over, the one named last changes fastest.
Arguments:
- sources: float32 [2, 2, 1024, 1024], P('depth', None, 'rows', 'shots'), may hold values from -6 to 6
- factor: float32 [2, 2, 1024, 1024], P('depth', None, ('rows', 'shots')), may hold values from -0.09375 to 0.09375
- block_mask: int32 [2, 2, 8, 8], P('depth'), may hold values 0 or 1
- inverse_diagonal: float32 [2, 2, 1024, 1024], P('depth', None, None, 'rows'), may hold values from -1.2 to 1.2, as said below
Outputs:
- solution: float32 [2, 2, 1024, 1024], P('depth', None, 'rows', 'shots')
Inputs may be any that keep to these rules, and one draw needn't show every extreme that they name: Each block inverse_diagonal[d, m] is lower triangular with diagonal entries between 0.8 and 1.2.
All inputs are finite; a program needn't handle non-finite values. No bound on the sum of `block_mask` on one device may be relied on, other than what follows from the above.
Results may differ from a plain program's by a relative error of at most 0.0001.
Values sent between devices are 32-bit elements; how exact they have to be, the bound alone decides.
No kernel may reach another device: no remote copies, remote signals or barrier semaphores. Data moves between devices by JAX's collectives and lax.ppermute only.
A program may use at most 64 MiB of HBM per device.

v0:
```python
import functools

import jax
import jax.numpy as jnp
from jax import lax
from jax.experimental import pallas as pl
from jax.experimental.pallas import tpu as pltpu
from jax.sharding import PartitionSpec as P


F32, BF16 = jnp.float32, jnp.bfloat16
VMEM = pl.BlockSpec(memory_space=pltpu.VMEM)
SMEM = pl.BlockSpec(memory_space=pltpu.SMEM)
GRANT = 12 * 1024 * 1024


def split(value):
    high = value.astype(BF16)
    return high, (value - high.astype(F32)).astype(BF16)


def beside(value):
    return jnp.concatenate(split(value), axis=1)


def mm(left, right, contract=((1,), (0,))):
    return lax.dot_general(left, right, (contract, ((), ())), preferred_element_type=F32)


def folded(left_high, left_low, right_pair, contract=((1,), (0,))):
    both = mm(left_high, right_pair, contract) + mm(left_low, right_pair, contract)
    width = both.shape[1] // 2
    return both[:, :width] + both[:, width:]


def part_of(array, *index):
    return array, index


def call(body, outs, ins, flops, scratch=()):
    arrays = [x[0] if isinstance(x, tuple) else x for x in ins]
    parts = [x[1] if isinstance(x, tuple) else None for x in ins]
    picked = [i for i, index in enumerate(parts) if index is not None]

    def specs(array, index):
        if index is not None:
            return pl.BlockSpec(memory_space=pltpu.HBM)
        return SMEM if array.dtype == jnp.int32 else VMEM

    def run(*refs):
        refs = list(refs)
        if picked:
            semaphores = refs.pop()
            buffers = [refs.pop() for _ in picked][::-1]
            copies = []
            for number, i in enumerate(picked):
                source = refs[i].at[parts[i]]
                copies.append(pltpu.make_async_copy(source, buffers[number], semaphores.at[number]))
                copies[-1].start()
                refs[i] = buffers[number]
            for copy in copies:
                copy.wait()
        body(*refs)

    held = [pltpu.VMEM(arrays[i].shape[len(parts[i]) :], arrays[i].dtype) for i in picked]
    if picked:
        held.append(pltpu.SemaphoreType.DMA((len(picked),)))
    moved = sum(x.size * x.dtype.itemsize for x in arrays)
    return pl.pallas_call(
        run,
        out_shape=[jax.ShapeDtypeStruct(shape, kind) for shape, kind in outs],
        in_specs=[specs(array, index) for array, index in zip(arrays, parts)],
        out_specs=[VMEM] * len(outs),
        scratch_shapes=list(scratch) + held,
        compiler_params=pltpu.CompilerParams(vmem_limit_bytes=GRANT),
        cost_estimate=pl.CostEstimate(flops=flops, bytes_accessed=moved, transcendentals=0),
    )(*arrays)


def spot(distance):
    count, index = lax.axis_size("shots"), lax.axis_index("shots")
    at = lax.rem(jnp.where(index % 2 == 0, index // 2, count - 1 - index // 2) + (distance + count), count)
    return jnp.where(2 * at < count, 2 * at, 2 * (count - 1 - at) + 1)


def share_rows(distance, share):
    return pl.ds(pl.multiple_of(spot(distance) * share, share), share)


def product(tiles, share, block, group, mask, factor, high, low, out):
    width = high.shape[0]
    first = ((group * lax.axis_size("shots") + lax.axis_index("shots")) * share) // block
    size = min(share, block)
    parts = []
    for tile in range(tiles):
        for band in range(share // size):
            pieces = []
            for column in range(width // block):
                keep = mask[0, tile, first + band, column].astype(F32)
                pieces.append(factor(tile, slice(band * size, (band + 1) * size), column * block, block) * keep)
            parts.append(jnp.concatenate(pieces, axis=1))
    stacked = jnp.concatenate(split(jnp.concatenate(parts, axis=0)), axis=0)
    both = mm(stacked, high[...]) + mm(stacked, low[...])
    out[...] = both[: tiles * share] + both[tiles * share :]


def first_body(tiles, share, block, mask, factor, inverse, own, out, high, low, pair):
    high[...], low[...] = split(inverse[...])
    pair[...] = beside(own[...])

    def load(tile, rows, start, size):
        return factor[tile, rows, start : start + size]

    product(tiles, share, block, lax.axis_index("rows"), mask, load, high, low, out)


def second_body(tiles, share, block, mask, left, right, high, low, inverse, out, three, corner):
    half = left.shape[2]
    quarter = half // 2
    three[0] = inverse[half : half + quarter, :quarter]
    three[1] = inverse[half + quarter :, :quarter]
    three[2] = inverse[half + quarter :, quarter:]
    corner[...] = inverse[half : half + quarter, quarter:]

    def load(tile, rows, start, size):
        side = left if start < half else right
        return side[tile, rows, start % half : start % half + size]

    product(tiles, share, block, 1 - lax.axis_index("rows"), mask, load, high, low, out)


def hop_body(tiles, share, distances, pair, level, *refs):
    count = len(distances)
    chunks, outs = refs[: 2 * count], refs[2 * count :]
    mine, theirs = outs[:2]
    flip, zero = lax.axis_index("rows"), lax.axis_index("depth") == 0
    rhs = pair[...]
    for group in range(2):
        block = jnp.concatenate([chunks[group * count + i][...] for i in range(count)], axis=0)
        outs[2 + 2 * group][...], outs[3 + 2 * group][...] = split(jnp.transpose(block))
        value = folded(*split(block), rhs)
        half_index = jnp.where(flip == 0, group, 1 - group)
        for i in range(count):
            first = value[(i * tiles) * share : (i * tiles + 1) * share]
            second = value[(i * tiles + 1) * share : (i * tiles + 2) * share]
            near = -jnp.where(zero, first, second)
            if group == 0:
                near = near + level[share_rows(distances[i], share), :]
            at = pl.ds(pl.multiple_of((i * 2 + half_index) * share, share), share)
            mine[at, :] = near
            theirs[at, :] = -jnp.where(zero, second, first)


def start_body(high, low, pair, out, lower):
    value = folded(high[...], low[...], pair[...])
    out[...] = value
    lower[...] = value[value.shape[0] // 2 :]


def base_body(high, low, part, far, out):
    half = far.shape[0]
    value = jnp.concatenate([part[:half, :], part[half:, :] + far[...]], axis=0)
    rows = jnp.concatenate(split(jnp.transpose(value)), axis=0)
    both = mm(rows, high[...]) + mm(rows, low[...])
    shots = both.shape[0] // 2
    out[...] = jnp.transpose(both[:shots] + both[shots:])


def square_body(inverse, three, corner, near_high, near_low, far_high, far_low):
    half = inverse.shape[1]
    high, low = split(inverse[...])
    turned_high, turned_low = jnp.transpose(high), jnp.transpose(low)
    near = mm(turned_high, high) + mm(turned_high, low) + mm(turned_low, high)
    near_high[...], near_low[...] = split(near)
    other = jnp.concatenate(
        [jnp.concatenate([three[0], corner[...]], axis=1), jnp.concatenate([three[1], three[2]], axis=1)], axis=0
    )
    other_high, other_low = split(other)
    turned_high, turned_low = turned_high[:, half:], turned_low[:, half:]
    far = mm(turned_high, other_high) + mm(turned_high, other_low) + mm(turned_low, other_high)
    far_high[...], far_low[...] = split(far)


def top_body(share, stages, near_high, near_low, far_high, far_low, *refs):
    batches = len(stages)
    sums, others, out, rest = refs[:batches], refs[batches : 2 * batches], refs[2 * batches], refs[2 * batches + 1]
    for number, distances in enumerate(stages):
        for i, distance in enumerate(distances):
            for group in range(2):
                rows = pl.ds((i * 2 + group) * share, share)
                rest[group, share_rows(distance, share), :] = sums[number][rows, :] + others[number][rows, :]
    flip = lax.axis_index("rows")
    out[...] = folded(near_high[...], near_low[...], beside(rest[flip])) + folded(
        far_high[...], far_low[...], beside(rest[1 - flip])
    )


def couple(tiles, share, stages, start, mine, peer, flats, both):
    depth = lax.axis_index("depth")
    both[depth] = mine[...]
    both[1 - depth] = peer[...]
    rows = [
        jnp.concatenate(
            [both[t, share_rows(distance, share), :] for distance in distances for t in range(tiles)], axis=0
        )
        for distances in stages
    ]
    highs, lows = [flat[...] for flat in flats[::2]], [flat[...] for flat in flats[1::2]]
    if all(flat.shape[1] % 128 == 0 for flat in highs):
        rows = [jnp.concatenate(rows, axis=0)]
        highs, lows = [jnp.concatenate(highs, axis=1)], [jnp.concatenate(lows, axis=1)]
    total = start[...]
    for high, low, row in zip(highs, lows, rows):
        total = total - folded(high, low, beside(row))
    return total


def couple_body(tiles, share, stages, start, mine, peer, *refs):
    *flats, out, both = refs
    out[...] = couple(tiles, share, stages, start, mine, peer, flats, both)


def final_body(tiles, share, stages, start, mine, peer, top, *refs):
    *flats, out, both = refs
    out[0, 1] = top[...]
    out[0, 0] = couple(tiles, share, stages, start, mine, peer, flats, both)


def snake(count):
    return list(range(0, count, 2)) + list(range(1, count, 2))[::-1]


def per_device(sources, factor, block_mask, inverse_diagonal):
    shots_count = lax.axis_size("shots")
    rows_count = lax.axis_size("rows")
    depth_count = lax.axis_size("depth")
    assert rows_count == 2 and depth_count == 2 and sources.shape[1] == 2 and shots_count % 2 == 0
    order = snake(shots_count)
    ahead = [(order[i], order[(i + 1) % shots_count]) for i in range(shots_count)]
    behind = [(b, a) for a, b in ahead]
    swap = [(0, 1), (1, 0)]

    tiles, share, width = factor.shape[1:]
    half = width // rows_count
    block = width // block_mask.shape[3]
    shots = sources.shape[3]
    quarter = half // 2

    far_right = lax.ppermute(factor[0, :, :, half:], "rows", swap)
    far_left = lax.ppermute(factor[0, :, :, :half], "rows", [(1, 0)])
    heavy = 8 * tiles * share * width * half
    chunk = ((tiles * share, half), F32)
    own, high0, low0, pair0 = call(
        functools.partial(first_body, tiles, share, block),
        [chunk] + [((width, half), BF16)] * 2 + [((half, 2 * shots), BF16)],
        [block_mask, part_of(factor, 0), part_of(inverse_diagonal, 0, 0), part_of(sources, 0, 0)],
        heavy,
    )
    far, three1, corner1 = call(
        functools.partial(second_body, tiles, share, block),
        [chunk, ((3, quarter, quarter), F32), ((quarter, quarter), F32)],
        [block_mask, far_left, far_right, high0, low0, part_of(inverse_diagonal, 0, 1)],
        heavy,
    )

    hops = shots_count // 2
    stages, pieces = [[0]], [[[own], [far]]]
    forward, backward = [own, far], [own, far]
    for hop in range(1, hops):
        for number in range(2):
            forward[number] = lax.ppermute(forward[number], "shots", ahead)
            backward[number] = lax.ppermute(backward[number], "shots", behind)
        if hop == 1:
            stages[0] += [-1, 1]
            for number in range(2):
                pieces[0][number] += [forward[number], backward[number]]
        else:
            stages.append([-hop, hop])
            pieces.append([list(pair) for pair in zip(forward, backward)])
    stages.append([hops])
    pieces.append([[lax.ppermute(forward[0], "shots", ahead)], [lax.ppermute(backward[1], "shots", behind)]])

    part0, lower0 = call(
        start_body, [((width, shots), F32), ((half, shots), F32)], [high0, low0, pair0], 8 * width * half * shots
    )
    far0 = lax.ppermute(lower0, "rows", swap)
    (base0,) = call(base_body, [((half, shots), F32)], [high0, low0, part0, far0], 8 * width * half * shots)

    squares = call(
        square_body,
        [((half, half), BF16)] * 4,
        [part_of(inverse_diagonal, 0, 1), lax.ppermute(three1, "rows", swap), lax.ppermute(corner1, "rows", [(0, 1)])],
        9 * half * half * half * 2,
    )

    sums, others, flats = [], [], [[], []]
    for distances, piece in zip(stages, pieces):
        count = len(distances)
        deep = count * tiles * share
        mine, theirs, *flat = call(
            functools.partial(hop_body, tiles, share, distances),
            [((2 * count * share, shots), F32)] * 2 + [((half, deep), BF16)] * 4,
            [pair0, part_of(sources, 0, 1)] + piece[0] + piece[1],
            16 * deep * half * shots,
        )
        total = mine + lax.ppermute(theirs, "depth", swap)
        sums.append(total)
        others.append(lax.ppermute(total, "rows", swap))
        flats[0] += flat[:2]
        flats[1] += flat[2:]

    (top,) = call(
        functools.partial(top_body, share, stages),
        [((half, shots), F32)],
        [*squares, *sums, *others],
        16 * half * half * shots,
        scratch=[pltpu.VMEM((2, half, shots), F32)],
    )
    far_top = lax.ppermute(top, "rows", swap)
    peer_top = lax.ppermute(top, "depth", swap)
    peer_far = lax.ppermute(far_top, "depth", swap)
    work = 8 * half * width * shots
    (almost,) = call(
        functools.partial(couple_body, tiles, share, stages),
        [((half, shots), F32)],
        [base0, top, peer_top, *flats[0]],
        work,
        scratch=[pltpu.VMEM((2, half, shots), F32)],
    )
    (answer,) = call(
        functools.partial(final_body, tiles, share, stages),
        [((1, 2, half, shots), F32)],
        [almost, far_top, peer_far, top, *flats[1]],
        work,
        scratch=[pltpu.VMEM((2, half, shots), F32)],
    )
    return answer


def solution(mesh):
    placed = (
        P("depth", None, "rows", "shots"),
        P("depth", None, ("rows", "shots"), None),
        P("depth", None, None, None),
        P("depth", None, None, "rows"),
    )

    return jax.shard_map(
        per_device,
        mesh=mesh,
        in_specs=placed,
        out_specs=P("depth", None, "rows", "shots"),
        check_vma=False,
    )
```

profile of v0, /device:TPU:0, one launch (start us, length us, event | category | flops | bytes accessed | tf_op | source)
XLA Modules:
  0.0 94.0 jit_solution(10172054619030940981)
XLA Ops:
  1.1 1.3 %collective-permute-start.1 = (f32[2,64,512]{2,1,0:T(8,128)S(1)}, f32[2,64,512]{2,1,0:T(8,128)S(1)}, u32[]{:S(2)}, u32[]{:S(2)}) collective-permute-start(f32[2,64,512]{2,1,0:T(8,128)S(1)} %get-tuple-element.80), channel_id=1, source_target_pairs={{8,0},{9,1},{10,2},{11,3},{12,4},{13,5},{14,6},{15,7},{24,16},{25,... | collective-permute-start | bytes 786440 | tf_op jit(solution)/shard_map/ppermute | solution.py:250
  2.4 3.0 %collective-permute-start.2 = (f32[2,64,512]{2,1,0:T(8,128)S(1)}, f32[2,64,512]{2,1,0:T(8,128)S(1)}, u32[]{:S(2)}, u32[]{:S(2)}) collective-permute-start(f32[2,64,512]{2,1,0:T(8,128)S(1)} %get-tuple-element.79), channel_id=1, source_target_pairs={{0,8},{8,0},{1,9},{9,1},{2,10},{10,2},{3,11},{11,3},{4,12},{12,4},... | collective-permute-start | bytes 786440 | tf_op jit(solution)/shard_map/ppermute | solution.py:249
  5.4 2.2 %copy-done = f32[1,2,1024,512]{3,2,1,0:T(8,128)S(1)} copy-done((f32[1,2,1024,512]{3,2,1,0:T(8,128)S(1)}, f32[1,2,1024,512]{3,2,1,0:T(8,128)}, u32[]{:S(2)}) %copy-start) | copy-done | bytes 4194328
  10.4 1.8 %shard_map.46 = (f32[128,512]{1,0:T(8,128)S(1)}, bf16[1024,512]{1,0:T(8,128)(2,1)S(1)}, bf16[1024,512]{1,0:T(8,128)(2,1)S(1)}, bf16[512,256]{1,0:T(8,128)(2,1)S(1)}) custom-call(s32[1,2,8,8]{3,2,1,0:T(8,128)S(1)} %copy-done.5, f32[1,2,64,1024]{3,2,1,0:T(8,128)S(1)} %copy-done.4, f32[1,2,1024,512]{3,2,1,0:T(8,128)S(1)} %copy-done, ...), custom_call_target="tpu_custom_call" | custom-call | flops 536870912 | bytes 5243392 | tf_op jit(solution)/shard_map/pallas_call | solution.py:69
  12.2 2.8 %collective-permute-start.5 = (f32[128,512]{1,0:T(8,128)S(1)}, f32[128,512]{1,0:T(8,128)S(1)}, u32[]{:S(2)}, u32[]{:S(2)}) collective-permute-start(f32[128,512]{1,0:T(8,128)S(1)} %get-tuple-element.53.refs_2_), channel_id=1, source_target_pairs={{0,2},{2,4},{4,6},{6,7},{7,5},{5,3},{3,1},{1,0},{8,10},{10,12},{12... | collective-permute-start | bytes 786440 | tf_op jit(solution)/shard_map/ppermute | solution.py:271
  14.9 2.3 %collective-permute-done.2.refs_2_ = f32[2,64,512]{2,1,0:T(8,128)S(1)} collective-permute-done((f32[2,64,512]{2,1,0:T(8,128)S(1)}, f32[2,64,512]{2,1,0:T(8,128)S(1)}, u32[]{:S(2)}, u32[]{:S(2)}) %collective-permute-start.2) | collective-permute-done | bytes 262176 | tf_op jit(solution)/shard_map/ppermute | solution.py:249
  17.3 1.6 %shard_map.49 = (f32[128,512]{1,0:T(8,128)S(1)}, f32[3,256,256]{2,1,0:T(8,128)S(1)}, f32[256,256]{1,0:T(8,128)S(1)}) custom-call(s32[1,2,8,8]{3,2,1,0:T(8,128)S(1)} %copy-done.5, f32[2,64,512]{2,1,0:T(8,128)S(1)} %collective-permute-done.1.refs_1_, f32[2,64,512]{2,1,0:T(8,128)S(1)} %collective-permute-done.2.refs_2_, ...), custom_call_target="tpu_custom_call" | custom-call | flops 536870912 | bytes 6816256 | tf_op jit(solution)/shard_map/pallas_call | solution.py:69
  18.9 2.4 %collective-permute-start.8 = (f32[128,512]{1,0:T(8,128)S(1)}, f32[128,512]{1,0:T(8,128)S(1)}, u32[]{:S(2)}, u32[]{:S(2)}) collective-permute-start(f32[128,512]{1,0:T(8,128)S(1)} %get-tuple-element.54.refs_5_), channel_id=1, source_target_pairs={{2,0},{4,2},{6,4},{7,6},{5,7},{3,5},{1,3},{0,1},{10,8},{12,10},{14... | collective-permute-start | bytes 786440 | tf_op jit(solution)/shard_map/ppermute | solution.py:272
  21.3 1.6 %collective-permute-start.6 = (f32[128,512]{1,0:T(8,128)S(1)}, f32[128,512]{1,0:T(8,128)S(1)}, u32[]{:S(2)}, u32[]{:S(2)}) collective-permute-start(f32[128,512]{1,0:T(8,128)S(1)} %get-tuple-element.53.refs_2_), channel_id=1, source_target_pairs={{2,0},{4,2},{6,4},{7,6},{5,7},{3,5},{1,3},{0,1},{10,8},{12,10},{14... | collective-permute-start | bytes 786440 | tf_op jit(solution)/shard_map/ppermute | solution.py:272
  23.4 5.1 %collective-permute-done.8.refs_7_ = f32[128,512]{1,0:T(8,128)S(1)} collective-permute-done((f32[128,512]{1,0:T(8,128)S(1)}, f32[128,512]{1,0:T(8,128)S(1)}, u32[]{:S(2)}, u32[]{:S(2)}) %collective-permute-start.8) | collective-permute-done | bytes 262176 | tf_op jit(solution)/shard_map/ppermute | solution.py:272
  28.5 2.0 %collective-permute-start.13 = (f32[128,512]{1,0:T(8,128)S(1)}, f32[128,512]{1,0:T(8,128)S(1)}, u32[]{:S(2)}, u32[]{:S(2)}) collective-permute-start(f32[128,512]{1,0:T(8,128)S(1)} %collective-permute-done.8.refs_7_), channel_id=1, source_target_pairs={{2,0},{4,2},{6,4},{7,6},{5,7},{3,5},{1,3},{0,1},{10,8},{12,10},{14... | collective-permute-start | bytes 786440 | tf_op jit(solution)/shard_map/ppermute | solution.py:272
  30.5 3.7 %collective-permute-done.6.refs_4_ = f32[128,512]{1,0:T(8,128)S(1)} collective-permute-done((f32[128,512]{1,0:T(8,128)S(1)}, f32[128,512]{1,0:T(8,128)S(1)}, u32[]{:S(2)}, u32[]{:S(2)}) %collective-permute-start.6) | collective-permute-done | bytes 262176 | tf_op jit(solution)/shard_map/ppermute | solution.py:272
  34.1 2.0 %collective-permute-start.11 = (f32[128,512]{1,0:T(8,128)S(1)}, f32[128,512]{1,0:T(8,128)S(1)}, u32[]{:S(2)}, u32[]{:S(2)}) collective-permute-start(f32[128,512]{1,0:T(8,128)S(1)} %collective-permute-done.6.refs_4_), channel_id=1, source_target_pairs={{2,0},{4,2},{6,4},{7,6},{5,7},{3,5},{1,3},{0,1},{10,8},{12,10},{14... | collective-permute-start | bytes 786440 | tf_op jit(solution)/shard_map/ppermute | solution.py:272
  36.1 2.0 %collective-permute-start.15 = (f32[128,512]{1,0:T(8,128)S(1)}, f32[128,512]{1,0:T(8,128)S(1)}, u32[]{:S(2)}, u32[]{:S(2)}) collective-permute-start(f32[128,512]{1,0:T(8,128)S(1)} %collective-permute-done.10.refs_2_), channel_id=1, source_target_pairs={{0,2},{2,4},{4,6},{6,7},{7,5},{5,3},{3,1},{1,0},{8,10},{10,12},{12... | collective-permute-start | bytes 786440 | tf_op jit(solution)/shard_map/ppermute | solution.py:271
  38.2 1.6 %collective-permute-done.13.refs_5_ = f32[128,512]{1,0:T(8,128)S(1)} collective-permute-done((f32[128,512]{1,0:T(8,128)S(1)}, f32[128,512]{1,0:T(8,128)S(1)}, u32[]{:S(2)}, u32[]{:S(2)}) %collective-permute-start.13) | collective-permute-done | bytes 262176 | tf_op jit(solution)/shard_map/ppermute | solution.py:272
  39.7 2.0 %collective-permute-start.18 = (f32[128,512]{1,0:T(8,128)S(1)}, f32[128,512]{1,0:T(8,128)S(1)}, u32[]{:S(2)}, u32[]{:S(2)}) collective-permute-start(f32[128,512]{1,0:T(8,128)S(1)} %collective-permute-done.13.refs_5_), channel_id=1, source_target_pairs={{2,0},{4,2},{6,4},{7,6},{5,7},{3,5},{1,3},{0,1},{10,8},{12,10},{14... | collective-permute-start | bytes 786440 | tf_op jit(solution)/shard_map/ppermute | solution.py:272
  41.7 3.7 %collective-permute-done.11.refs_3_ = f32[128,512]{1,0:T(8,128)S(1)} collective-permute-done((f32[128,512]{1,0:T(8,128)S(1)}, f32[128,512]{1,0:T(8,128)S(1)}, u32[]{:S(2)}, u32[]{:S(2)}) %collective-permute-start.11) | collective-permute-done | bytes 262176 | tf_op jit(solution)/shard_map/ppermute | solution.py:272
  45.3 2.0 %collective-permute-start.16 = (f32[128,512]{1,0:T(8,128)S(1)}, f32[128,512]{1,0:T(8,128)S(1)}, u32[]{:S(2)}, u32[]{:S(2)}) collective-permute-start(f32[128,512]{1,0:T(8,128)S(1)} %collective-permute-done.11.refs_3_), channel_id=1, source_target_pairs={{2,0},{4,2},{6,4},{7,6},{5,7},{3,5},{1,3},{0,1},{10,8},{12,10},{14... | collective-permute-start | bytes 786440 | tf_op jit(solution)/shard_map/ppermute | solution.py:272
  47.4 2.0 %collective-permute-start.20 = (f32[128,512]{1,0:T(8,128)S(1)}, f32[128,512]{1,0:T(8,128)S(1)}, u32[]{:S(2)}, u32[]{:S(2)}) collective-permute-start(f32[128,512]{1,0:T(8,128)S(1)} %collective-permute-done.15.refs_2_), channel_id=1, source_target_pairs={{0,2},{2,4},{4,6},{6,7},{7,5},{5,3},{3,1},{1,0},{8,10},{10,12},{12... | collective-permute-start | bytes 786440 | tf_op jit(solution)/shard_map/ppermute | solution.py:281
  49.4 1.6 %collective-permute-done.18.refs_5_ = f32[128,512]{1,0:T(8,128)S(1)} collective-permute-done((f32[128,512]{1,0:T(8,128)S(1)}, f32[128,512]{1,0:T(8,128)S(1)}, u32[]{:S(2)}, u32[]{:S(2)}) %collective-permute-start.18) | collective-permute-done | bytes 262176 | tf_op jit(solution)/shard_map/ppermute | solution.py:272
  51.0 2.0 %collective-permute-start.21 = (f32[128,512]{1,0:T(8,128)S(1)}, f32[128,512]{1,0:T(8,128)S(1)}, u32[]{:S(2)}, u32[]{:S(2)}) collective-permute-start(f32[128,512]{1,0:T(8,128)S(1)} %collective-permute-done.18.refs_5_), channel_id=1, source_target_pairs={{2,0},{4,2},{6,4},{7,6},{5,7},{3,5},{1,3},{0,1},{10,8},{12,10},{14... | collective-permute-start | bytes 786440 | tf_op jit(solution)/shard_map/ppermute | solution.py:281
  53.6 3.0 %collective-permute-done.16.refs_3_ = f32[128,512]{1,0:T(8,128)S(1)} collective-permute-done((f32[128,512]{1,0:T(8,128)S(1)}, f32[128,512]{1,0:T(8,128)S(1)}, u32[]{:S(2)}, u32[]{:S(2)}) %collective-permute-start.16) | collective-permute-done | bytes 262176 | tf_op jit(solution)/shard_map/ppermute | solution.py:272
  56.6 1.5 %collective-permute-start.4 = (f32[256,256]{1,0:T(8,128)S(1)}, f32[256,256]{1,0:T(8,128)S(1)}, u32[]{:S(2)}, u32[]{:S(2)}) collective-permute-start(f32[256,256]{1,0:T(8,128)S(1)} %get-tuple-element.48), channel_id=1, source_target_pairs={{0,8},{1,9},{2,10},{3,11},{4,12},{5,13},{6,14},{7,15},{16,24},{17,... | collective-permute-start | bytes 786440 | tf_op jit(solution)/shard_map/ppermute | solution.py:292
  61.8 1.8 %collective-permute-start.24 = (f32[256,128]{1,0:T(8,128)S(1)}, f32[256,128]{1,0:T(8,128)S(1)}, u32[]{:S(2)}, u32[]{:S(2)}) collective-permute-start(f32[256,128]{1,0:T(8,128)S(1)} %add.13.refs_5_), channel_id=1, source_target_pairs={{0,8},{8,0},{1,9},{9,1},{2,10},{10,2},{3,11},{11,3},{4,12},{12,4},... | collective-permute-start | bytes 393224 | tf_op jit(solution)/shard_map/ppermute | solution.py:308
  64.7 2.5 %collective-permute-start.26 = (f32[128,128]{1,0:T(8,128)S(1)}, f32[128,128]{1,0:T(8,128)S(1)}, u32[]{:S(2)}, u32[]{:S(2)}) collective-permute-start(f32[128,128]{1,0:T(8,128)S(1)} %add.15.refs_7_), channel_id=1, source_target_pairs={{0,8},{8,0},{1,9},{9,1},{2,10},{10,2},{3,11},{11,3},{4,12},{12,4},... | collective-permute-start | bytes 196616 | tf_op jit(solution)/shard_map/ppermute | solution.py:308
  67.2 2.8 %shard_map.50 = (bf16[512,512]{1,0:T(8,128)(2,1)S(1)}, bf16[512,512]{1,0:T(8,128)(2,1)S(1)}, bf16[512,512]{1,0:T(8,128)(2,1)S(1)}, bf16[512,512]{1,0:T(8,128)(2,1)S(1)}) custom-call(f32[1,2,1024,512]{3,2,1,0:T(8,128)S(1)} %copy-done.1, f32[3,256,256]{2,1,0:T(8,128)S(1)} %collective-permute-done.3.refs_1_, f32[256,256]{1,0:T(8,128)S(1)} %collective-permute-done.4.refs_2_), custom_call_target="tpu_custom_call" | custom-call | flops 2415919104 | bytes 5242880 | tf_op jit(solution)/shard_map/pallas_call | solution.py:69
  70.0 2.1 %collective-permute-done.24.refs_9_ = f32[256,128]{1,0:T(8,128)S(1)} collective-permute-done((f32[256,128]{1,0:T(8,128)S(1)}, f32[256,128]{1,0:T(8,128)S(1)}, u32[]{:S(2)}, u32[]{:S(2)}) %collective-permute-start.24) | collective-permute-done | bytes 131104 | tf_op jit(solution)/shard_map/ppermute | solution.py:308
  72.1 2.6 %collective-permute-done.25.refs_10_ = f32[256,128]{1,0:T(8,128)S(1)} collective-permute-done((f32[256,128]{1,0:T(8,128)S(1)}, f32[256,128]{1,0:T(8,128)S(1)}, u32[]{:S(2)}, u32[]{:S(2)}) %collective-permute-start.25) | collective-permute-done | bytes 131104 | tf_op jit(solution)/shard_map/ppermute | solution.py:308
  76.4 2.5 %collective-permute-start.28 = (f32[512,128]{1,0:T(8,128)S(1)}, f32[512,128]{1,0:T(8,128)S(1)}, u32[]{:S(2)}, u32[]{:S(2)}) collective-permute-start(f32[512,128]{1,0:T(8,128)S(1)} %shard_map.55.refs_1_.refs_3_), channel_id=1, source_target_pairs={{0,8},{8,0},{1,9},{9,1},{2,10},{10,2},{3,11},{11,3},{4,12},{12,4},... | collective-permute-start | bytes 786440 | tf_op jit(solution)/shard_map/ppermute | solution.py:319
  79.8 6.3 %collective-permute-done.28.refs_1_ = f32[512,128]{1,0:T(8,128)S(1)} collective-permute-done((f32[512,128]{1,0:T(8,128)S(1)}, f32[512,128]{1,0:T(8,128)S(1)}, u32[]{:S(2)}, u32[]{:S(2)}) %collective-permute-start.28) | collective-permute-done | bytes 262176 | tf_op jit(solution)/shard_map/ppermute | solution.py:319
  86.1 4.7 %collective-permute-done.refs_3_ = f32[512,128]{1,0:T(8,128)S(1)} collective-permute-done((f32[512,128]{1,0:T(8,128)S(1)}, f32[512,128]{1,0:T(8,128)S(1)}, u32[]{:S(2)}, u32[]{:S(2)}) %collective-permute-start) | collective-permute-done | bytes 262176 | tf_op jit(solution)/shard_map/ppermute | solution.py:286
  92.4 1.6 %shard_map.57 = f32[1,2,512,128]{3,2,1,0:T(8,128)} custom-call(f32[512,128]{1,0:T(8,128)S(1)} %shard_map.56.refs_0_, f32[512,128]{1,0:T(8,128)S(1)} %collective-permute-done.28.refs_1_, f32[512,128]{1,0:T(8,128)S(1)} %collective-permute-done.29.refs_2_, f32[512,128]{1,0:T(8,128)S(1)} %shard_map.55.refs_1_.refs_3_, ...), custom_call_target="tpu_custom_call" | custom-call | flops 536870912 | bytes 3145728 | tf_op jit(solution)/shard_map/pallas_call | solution.py:69
  (57 shorter events, 14.2 us)
Async XLA Ops:
  1.1 13.9 %collective-permute-start.1 = (f32[2,64,512]{2,1,0:T(8,128)S(1)}, f32[2,64,512]{2,1,0:T(8,128)S(1)}, u32[]{:S(2)}, u32[]{:S(2)}) collective-permute-start(f32[2,64,512]{2,1,0:T(8,128)S(1)} %get-tuple-element.80), channel_id=1, source_target_pairs={{8,0},{9,1},{10,2},{11,3},{12,4},{13,5},{14,6},{15,7},{24,16},{25,... | collective-permute-start | bytes 786440 | tf_op jit(solution)/shard_map/ppermute | solution.py:250
  2.4 14.9 %collective-permute-start.2 = (f32[2,64,512]{2,1,0:T(8,128)S(1)}, f32[2,64,512]{2,1,0:T(8,128)S(1)}, u32[]{:S(2)}, u32[]{:S(2)}) collective-permute-start(f32[2,64,512]{2,1,0:T(8,128)S(1)} %get-tuple-element.79), channel_id=1, source_target_pairs={{0,8},{8,0},{1,9},{9,1},{2,10},{10,2},{3,11},{11,3},{4,12},{12,4},... | collective-permute-start | bytes 786440 | tf_op jit(solution)/shard_map/ppermute | solution.py:249
  10.4 6.9 %copy-start.1 = (f32[1,2,1024,512]{3,2,1,0:T(8,128)S(1)}, f32[1,2,1024,512]{3,2,1,0:T(8,128)}, u32[]{:S(2)}) copy-start(f32[1,2,1024,512]{3,2,1,0:T(8,128)} %refs_0_.5) | copy-start | bytes 12582916
  12.1 40.8 %copy-start.3 = (f32[1,2,512,128]{3,2,1,0:T(8,128)S(1)}, f32[1,2,512,128]{3,2,1,0:T(8,128)}, u32[]{:S(2)}) copy-start(f32[1,2,512,128]{3,2,1,0:T(8,128)} %refs_1_.9) | copy-start | bytes 1572868
  12.2 11.1 %collective-permute-start.5 = (f32[128,512]{1,0:T(8,128)S(1)}, f32[128,512]{1,0:T(8,128)S(1)}, u32[]{:S(2)}, u32[]{:S(2)}) collective-permute-start(f32[128,512]{1,0:T(8,128)S(1)} %get-tuple-element.53.refs_2_), channel_id=1, source_target_pairs={{0,2},{2,4},{4,6},{6,7},{7,5},{5,3},{3,1},{1,0},{8,10},{10,12},{12... | collective-permute-start | bytes 786440 | tf_op jit(solution)/shard_map/ppermute | solution.py:271
  18.9 9.6 %collective-permute-start.8 = (f32[128,512]{1,0:T(8,128)S(1)}, f32[128,512]{1,0:T(8,128)S(1)}, u32[]{:S(2)}, u32[]{:S(2)}) collective-permute-start(f32[128,512]{1,0:T(8,128)S(1)} %get-tuple-element.54.refs_5_), channel_id=1, source_target_pairs={{2,0},{4,2},{6,4},{7,6},{5,7},{3,5},{1,3},{0,1},{10,8},{12,10},{14... | collective-permute-start | bytes 786440 | tf_op jit(solution)/shard_map/ppermute | solution.py:272
  21.3 12.8 %collective-permute-start.6 = (f32[128,512]{1,0:T(8,128)S(1)}, f32[128,512]{1,0:T(8,128)S(1)}, u32[]{:S(2)}, u32[]{:S(2)}) collective-permute-start(f32[128,512]{1,0:T(8,128)S(1)} %get-tuple-element.53.refs_2_), channel_id=1, source_target_pairs={{2,0},{4,2},{6,4},{7,6},{5,7},{3,5},{1,3},{0,1},{10,8},{12,10},{14... | collective-permute-start | bytes 786440 | tf_op jit(solution)/shard_map/ppermute | solution.py:272
  22.9 13.2 %collective-permute-start.7 = (f32[128,512]{1,0:T(8,128)S(1)}, f32[128,512]{1,0:T(8,128)S(1)}, u32[]{:S(2)}, u32[]{:S(2)}) collective-permute-start(f32[128,512]{1,0:T(8,128)S(1)} %get-tuple-element.54.refs_5_), channel_id=1, source_target_pairs={{0,2},{2,4},{4,6},{6,7},{7,5},{5,3},{3,1},{1,0},{8,10},{10,12},{12... | collective-permute-start | bytes 786440 | tf_op jit(solution)/shard_map/ppermute | solution.py:271
  23.3 12.8 %collective-permute-start.10 = (f32[128,512]{1,0:T(8,128)S(1)}, f32[128,512]{1,0:T(8,128)S(1)}, u32[]{:S(2)}, u32[]{:S(2)}) collective-permute-start(f32[128,512]{1,0:T(8,128)S(1)} %collective-permute-done.5.refs_3_), channel_id=1, source_target_pairs={{0,2},{2,4},{4,6},{6,7},{7,5},{5,3},{3,1},{1,0},{8,10},{10,12},{12... | collective-permute-start | bytes 786440 | tf_op jit(solution)/shard_map/ppermute | solution.py:271
  28.5 11.2 %collective-permute-start.13 = (f32[128,512]{1,0:T(8,128)S(1)}, f32[128,512]{1,0:T(8,128)S(1)}, u32[]{:S(2)}, u32[]{:S(2)}) collective-permute-start(f32[128,512]{1,0:T(8,128)S(1)} %collective-permute-done.8.refs_7_), channel_id=1, source_target_pairs={{2,0},{4,2},{6,4},{7,6},{5,7},{3,5},{1,3},{0,1},{10,8},{12,10},{14... | collective-permute-start | bytes 786440 | tf_op jit(solution)/shard_map/ppermute | solution.py:272
  34.1 11.2 %collective-permute-start.11 = (f32[128,512]{1,0:T(8,128)S(1)}, f32[128,512]{1,0:T(8,128)S(1)}, u32[]{:S(2)}, u32[]{:S(2)}) collective-permute-start(f32[128,512]{1,0:T(8,128)S(1)} %collective-permute-done.6.refs_4_), channel_id=1, source_target_pairs={{2,0},{4,2},{6,4},{7,6},{5,7},{3,5},{1,3},{0,1},{10,8},{12,10},{14... | collective-permute-start | bytes 786440 | tf_op jit(solution)/shard_map/ppermute | solution.py:272
  36.1 11.2 %collective-permute-start.12 = (f32[128,512]{1,0:T(8,128)S(1)}, f32[128,512]{1,0:T(8,128)S(1)}, u32[]{:S(2)}, u32[]{:S(2)}) collective-permute-start(f32[128,512]{1,0:T(8,128)S(1)} %collective-permute-done.7.refs_6_), channel_id=1, source_target_pairs={{0,2},{2,4},{4,6},{6,7},{7,5},{5,3},{3,1},{1,0},{8,10},{10,12},{12... | collective-permute-start | bytes 786440 | tf_op jit(solution)/shard_map/ppermute | solution.py:271
  36.1 31.1 %collective-permute-start.3 = (f32[3,256,256]{2,1,0:T(8,128)S(1)}, f32[3,256,256]{2,1,0:T(8,128)S(1)}, u32[]{:S(2)}, u32[]{:S(2)}) collective-permute-start(f32[3,256,256]{2,1,0:T(8,128)S(1)} %get-tuple-element.47), channel_id=1, source_target_pairs={{0,8},{8,0},{1,9},{9,1},{2,10},{10,2},{3,11},{11,3},{4,12},{12,4},... | collective-permute-start | bytes 2359304 | tf_op jit(solution)/shard_map/ppermute | solution.py:292
  36.1 11.2 %collective-permute-start.15 = (f32[128,512]{1,0:T(8,128)S(1)}, f32[128,512]{1,0:T(8,128)S(1)}, u32[]{:S(2)}, u32[]{:S(2)}) collective-permute-start(f32[128,512]{1,0:T(8,128)S(1)} %collective-permute-done.10.refs_2_), channel_id=1, source_target_pairs={{0,2},{2,4},{4,6},{6,7},{7,5},{5,3},{3,1},{1,0},{8,10},{10,12},{12... | collective-permute-start | bytes 786440 | tf_op jit(solution)/shard_map/ppermute | solution.py:271
  39.7 11.2 %collective-permute-start.18 = (f32[128,512]{1,0:T(8,128)S(1)}, f32[128,512]{1,0:T(8,128)S(1)}, u32[]{:S(2)}, u32[]{:S(2)}) collective-permute-start(f32[128,512]{1,0:T(8,128)S(1)} %collective-permute-done.13.refs_5_), channel_id=1, source_target_pairs={{2,0},{4,2},{6,4},{7,6},{5,7},{3,5},{1,3},{0,1},{10,8},{12,10},{14... | collective-permute-start | bytes 786440 | tf_op jit(solution)/shard_map/ppermute | solution.py:272
  45.3 11.2 %collective-permute-start.16 = (f32[128,512]{1,0:T(8,128)S(1)}, f32[128,512]{1,0:T(8,128)S(1)}, u32[]{:S(2)}, u32[]{:S(2)}) collective-permute-start(f32[128,512]{1,0:T(8,128)S(1)} %collective-permute-done.11.refs_3_), channel_id=1, source_target_pairs={{2,0},{4,2},{6,4},{7,6},{5,7},{3,5},{1,3},{0,1},{10,8},{12,10},{14... | collective-permute-start | bytes 786440 | tf_op jit(solution)/shard_map/ppermute | solution.py:272
  47.3 9.3 %collective-permute-start.17 = (f32[128,512]{1,0:T(8,128)S(1)}, f32[128,512]{1,0:T(8,128)S(1)}, u32[]{:S(2)}, u32[]{:S(2)}) collective-permute-start(f32[128,512]{1,0:T(8,128)S(1)} %collective-permute-done.12.refs_4_), channel_id=1, source_target_pairs={{0,2},{2,4},{4,6},{6,7},{7,5},{5,3},{3,1},{1,0},{8,10},{10,12},{12... | collective-permute-start | bytes 786440 | tf_op jit(solution)/shard_map/ppermute | solution.py:271
  47.4 11.2 %collective-permute-start.20 = (f32[128,512]{1,0:T(8,128)S(1)}, f32[128,512]{1,0:T(8,128)S(1)}, u32[]{:S(2)}, u32[]{:S(2)}) collective-permute-start(f32[128,512]{1,0:T(8,128)S(1)} %collective-permute-done.15.refs_2_), channel_id=1, source_target_pairs={{0,2},{2,4},{4,6},{6,7},{7,5},{5,3},{3,1},{1,0},{8,10},{10,12},{12... | collective-permute-start | bytes 786440 | tf_op jit(solution)/shard_map/ppermute | solution.py:281
  51.0 9.5 %collective-permute-start.21 = (f32[128,512]{1,0:T(8,128)S(1)}, f32[128,512]{1,0:T(8,128)S(1)}, u32[]{:S(2)}, u32[]{:S(2)}) collective-permute-start(f32[128,512]{1,0:T(8,128)S(1)} %collective-permute-done.18.refs_5_), channel_id=1, source_target_pairs={{2,0},{4,2},{6,4},{7,6},{5,7},{3,5},{1,3},{0,1},{10,8},{12,10},{14... | collective-permute-start | bytes 786440 | tf_op jit(solution)/shard_map/ppermute | solution.py:281
  56.6 4.3 %collective-permute-start.9 = (f32[384,128]{1,0:T(8,128)S(1)}, f32[384,128]{1,0:T(8,128)S(1)}, u32[]{:S(2)}, u32[]{:S(2)}) collective-permute-start(f32[384,128]{1,0:T(8,128)S(1)} %get-tuple-element.56), channel_id=1, source_target_pairs={{0,16},{16,0},{1,17},{17,1},{2,18},{18,2},{3,19},{19,3},{4,20},{20... | collective-permute-start | bytes 589832 | tf_op jit(solution)/shard_map/ppermute | solution.py:306
  56.6 8.1 %collective-permute-start.4 = (f32[256,256]{1,0:T(8,128)S(1)}, f32[256,256]{1,0:T(8,128)S(1)}, u32[]{:S(2)}, u32[]{:S(2)}) collective-permute-start(f32[256,256]{1,0:T(8,128)S(1)} %get-tuple-element.48), channel_id=1, source_target_pairs={{0,8},{1,9},{2,10},{3,11},{4,12},{5,13},{6,14},{7,15},{16,24},{17,... | collective-permute-start | bytes 786440 | tf_op jit(solution)/shard_map/ppermute | solution.py:292
  58.6 2.9 %collective-permute-start.14 = (f32[256,128]{1,0:T(8,128)S(1)}, f32[256,128]{1,0:T(8,128)S(1)}, u32[]{:S(2)}, u32[]{:S(2)}) collective-permute-start(f32[256,128]{1,0:T(8,128)S(1)} %get-tuple-element.58), channel_id=1, source_target_pairs={{0,16},{16,0},{1,17},{17,1},{2,18},{18,2},{3,19},{19,3},{4,20},{20... | collective-permute-start | bytes 393224 | tf_op jit(solution)/shard_map/ppermute | solution.py:306
  60.5 1.3 %collective-permute-start.19 = (f32[256,128]{1,0:T(8,128)S(1)}, f32[256,128]{1,0:T(8,128)S(1)}, u32[]{:S(2)}, u32[]{:S(2)}) collective-permute-start(f32[256,128]{1,0:T(8,128)S(1)} %get-tuple-element.60), channel_id=1, source_target_pairs={{0,16},{16,0},{1,17},{17,1},{2,18},{18,2},{3,19},{19,3},{4,20},{20... | collective-permute-start | bytes 393224 | tf_op jit(solution)/shard_map/ppermute | solution.py:306
  60.9 2.8 %collective-permute-start.22 = (f32[128,128]{1,0:T(8,128)S(1)}, f32[128,128]{1,0:T(8,128)S(1)}, u32[]{:S(2)}, u32[]{:S(2)}) collective-permute-start(f32[128,128]{1,0:T(8,128)S(1)} %get-tuple-element.62), channel_id=1, source_target_pairs={{0,16},{16,0},{1,17},{17,1},{2,18},{18,2},{3,19},{19,3},{4,20},{20... | collective-permute-start | bytes 196616 | tf_op jit(solution)/shard_map/ppermute | solution.py:306
  61.5 8.5 %collective-permute-start.23 = (f32[384,128]{1,0:T(8,128)S(1)}, f32[384,128]{1,0:T(8,128)S(1)}, u32[]{:S(2)}, u32[]{:S(2)}) collective-permute-start(f32[384,128]{1,0:T(8,128)S(1)} %add.12.refs_4_), channel_id=1, source_target_pairs={{0,8},{8,0},{1,9},{9,1},{2,10},{10,2},{3,11},{11,3},{4,12},{12,4},... | collective-permute-start | bytes 589832 | tf_op jit(solution)/shard_map/ppermute | solution.py:308
  61.8 10.3 %collective-permute-start.24 = (f32[256,128]{1,0:T(8,128)S(1)}, f32[256,128]{1,0:T(8,128)S(1)}, u32[]{:S(2)}, u32[]{:S(2)}) collective-permute-start(f32[256,128]{1,0:T(8,128)S(1)} %add.13.refs_5_), channel_id=1, source_target_pairs={{0,8},{8,0},{1,9},{9,1},{2,10},{10,2},{3,11},{11,3},{4,12},{12,4},... | collective-permute-start | bytes 393224 | tf_op jit(solution)/shard_map/ppermute | solution.py:308
  63.7 11.0 %collective-permute-start.25 = (f32[256,128]{1,0:T(8,128)S(1)}, f32[256,128]{1,0:T(8,128)S(1)}, u32[]{:S(2)}, u32[]{:S(2)}) collective-permute-start(f32[256,128]{1,0:T(8,128)S(1)} %add.14.refs_6_), channel_id=1, source_target_pairs={{0,8},{8,0},{1,9},{9,1},{2,10},{10,2},{3,11},{11,3},{4,12},{12,4},... | collective-permute-start | bytes 393224 | tf_op jit(solution)/shard_map/ppermute | solution.py:308
  64.7 10.9 %collective-permute-start.26 = (f32[128,128]{1,0:T(8,128)S(1)}, f32[128,128]{1,0:T(8,128)S(1)}, u32[]{:S(2)}, u32[]{:S(2)}) collective-permute-start(f32[128,128]{1,0:T(8,128)S(1)} %add.15.refs_7_), channel_id=1, source_target_pairs={{0,8},{8,0},{1,9},{9,1},{2,10},{10,2},{3,11},{11,3},{4,12},{12,4},... | collective-permute-start | bytes 196616 | tf_op jit(solution)/shard_map/ppermute | solution.py:308
  76.4 9.7 %collective-permute-start.28 = (f32[512,128]{1,0:T(8,128)S(1)}, f32[512,128]{1,0:T(8,128)S(1)}, u32[]{:S(2)}, u32[]{:S(2)}) collective-permute-start(f32[512,128]{1,0:T(8,128)S(1)} %shard_map.55.refs_1_.refs_3_), channel_id=1, source_target_pairs={{0,8},{8,0},{1,9},{9,1},{2,10},{10,2},{3,11},{11,3},{4,12},{12,4},... | collective-permute-start | bytes 786440 | tf_op jit(solution)/shard_map/ppermute | solution.py:319
  79.6 11.2 %collective-permute-start = (f32[512,128]{1,0:T(8,128)S(1)}, f32[512,128]{1,0:T(8,128)S(1)}, u32[]{:S(2)}, u32[]{:S(2)}) collective-permute-start(f32[512,128]{1,0:T(8,128)S(1)} %get-tuple-element.46), channel_id=1, source_target_pairs={{0,8},{8,0},{1,9},{9,1},{2,10},{10,2},{3,11},{11,3},{4,12},{12,4},... | collective-permute-start | bytes 786440 | tf_op jit(solution)/shard_map/ppermute | solution.py:286
  79.7 11.9 %collective-permute-start.27 = (f32[512,128]{1,0:T(8,128)S(1)}, f32[512,128]{1,0:T(8,128)S(1)}, u32[]{:S(2)}, u32[]{:S(2)}) collective-permute-start(f32[512,128]{1,0:T(8,128)S(1)} %shard_map.55.refs_1_.refs_3_), channel_id=1, source_target_pairs={{0,16},{16,0},{1,17},{17,1},{2,18},{18,2},{3,19},{19,3},{4,20},{20... | collective-permute-start | bytes 786440 | tf_op jit(solution)/shard_map/ppermute | solution.py:320
  86.1 6.3 %collective-permute-start.29 = (f32[512,128]{1,0:T(8,128)S(1)}, f32[512,128]{1,0:T(8,128)S(1)}, u32[]{:S(2)}, u32[]{:S(2)}) collective-permute-start(f32[512,128]{1,0:T(8,128)S(1)} %collective-permute-done.28.refs_1_), channel_id=1, source_target_pairs={{0,16},{16,0},{1,17},{17,1},{2,18},{18,2},{3,19},{19,3},{4,20},{20... | collective-permute-start | bytes 786440 | tf_op jit(solution)/shard_map/ppermute | solution.py:321
  (4 other events, 5.0 us)
where the time goes:
time: 94.3 us; the launch traced here: 94 us
  waiting for transfers between devices  39.4 us (42%)
  starting transfers between devices  35.4 us (38%)
  Pallas kernels  12.9 us (14%)
  local copies, waits for them, and re-layouts  6.04 us (6%)
    ppermute x6, waiting for transfers between devices, per_device(): backward[number] = lax.ppermute(backward[number], 'shots', behind)  18.4 us
    pallas_call x12, Pallas kernels, call(): pl.pallas_call(run, out_shape=[jax.ShapeDtypeStruct(shape, kind) for shap...  12.9 us
    ppermute x6, starting transfers between devices, per_device(): backward[number] = lax.ppermute(backward[number], 'shots', behind)  11.8 us
    ppermute x1, waiting for transfers between devices, per_device(): far_top = lax.ppermute(top, 'rows', swap)  6.29 us
    ppermute x4, waiting for transfers between devices, per_device(): others.append(lax.ppermute(total, 'rows', swap))  5.59 us
    ppermute x6, starting transfers between devices, per_device(): forward[number] = lax.ppermute(forward[number], 'shots', ahead)  5.5 us
    unnamed x12, local copies, waits for them, and re-layouts  4.98 us
    ppermute x1, waiting for transfers between devices, per_device(): far0 = lax.ppermute(lower0, 'rows', swap)  4.7 us
  transfers between devices with their start and end apart: 30, of which 15 were waited for; matrix products, arithmetic and copies ran while one was open for 0% of the time, Pallas kernels for 11%

commit v1 on v0

--- a/solution.py
+++ b/solution.py
@@ -10,7 +10,7 @@
 
 F32, BF16 = jnp.float32, jnp.bfloat16
 VMEM = pl.BlockSpec(memory_space=pltpu.VMEM)
-SMEM = pl.BlockSpec(memory_space=pltpu.SMEM)
+HBM = pl.BlockSpec(memory_space=pltpu.HBM)
 GRANT = 12 * 1024 * 1024
 
 
@@ -37,15 +37,13 @@
     return array, index
 
 
-def call(body, outs, ins, flops, scratch=()):
-    arrays = [x[0] if isinstance(x, tuple) else x for x in ins]
+def call(body, outs, ins, flops, scratch=(), plain=(), placed=(), alias=None):
+    arrays = [pltpu.with_memory_space_constraint(x[0], pltpu.HBM) if isinstance(x, tuple) else x for x in ins]
     parts = [x[1] if isinstance(x, tuple) else None for x in ins]
     picked = [i for i, index in enumerate(parts) if index is not None]
 
-    def specs(array, index):
-        if index is not None:
-            return pl.BlockSpec(memory_space=pltpu.HBM)
-        return SMEM if array.dtype == jnp.int32 else VMEM
+    def space(array):
+        return pltpu.SMEM if array.dtype == jnp.int32 else pltpu.VMEM
 
     def run(*refs):
         refs = list(refs)
@@ -62,16 +60,17 @@
                 copy.wait()
         body(*refs)
 
-    held = [pltpu.VMEM(arrays[i].shape[len(parts[i]) :], arrays[i].dtype) for i in picked]
+    held = [space(arrays[i])(arrays[i].shape[len(parts[i]) :], arrays[i].dtype) for i in picked]
     if picked:
         held.append(pltpu.SemaphoreType.DMA((len(picked),)))
     moved = sum(x.size * x.dtype.itemsize for x in arrays)
     return pl.pallas_call(
         run,
         out_shape=[jax.ShapeDtypeStruct(shape, kind) for shape, kind in outs],
-        in_specs=[specs(array, index) for array, index in zip(arrays, parts)],
-        out_specs=[VMEM] * len(outs),
+        in_specs=[HBM if index is not None or i in plain else VMEM for i, index in enumerate(parts)],
+        out_specs=[HBM if i in placed else VMEM for i in range(len(outs))],
         scratch_shapes=list(scratch) + held,
+        input_output_aliases=alias or {},
         compiler_params=pltpu.CompilerParams(vmem_limit_bytes=GRANT),
         cost_estimate=pl.CostEstimate(flops=flops, bytes_accessed=moved, transcendentals=0),
     )(*arrays)
@@ -92,16 +91,16 @@
     first = ((group * lax.axis_size("shots") + lax.axis_index("shots")) * share) // block
     size = min(share, block)
     parts = []
-    for tile in range(tiles):
+    for tile in tiles:
         for band in range(share // size):
             pieces = []
             for column in range(width // block):
-                keep = mask[0, tile, first + band, column].astype(F32)
+                keep = mask[tile, first + band, column].astype(F32)
                 pieces.append(factor(tile, slice(band * size, (band + 1) * size), column * block, block) * keep)
             parts.append(jnp.concatenate(pieces, axis=1))
     stacked = jnp.concatenate(split(jnp.concatenate(parts, axis=0)), axis=0)
     both = mm(stacked, high[...]) + mm(stacked, low[...])
-    out[...] = both[: tiles * share] + both[tiles * share :]
+    out[...] = both[: len(tiles) * share] + both[len(tiles) * share :]
 
 
 def first_body(tiles, share, block, mask, factor, inverse, own, out, high, low, pair):
@@ -111,32 +110,40 @@
     def load(tile, rows, start, size):
         return factor[tile, rows, start : start + size]
 
-    product(tiles, share, block, lax.axis_index("rows"), mask, load, high, low, out)
-
-
-def second_body(tiles, share, block, mask, left, right, high, low, inverse, out, three, corner):
-    half = left.shape[2]
-    quarter = half // 2
-    three[0] = inverse[half : half + quarter, :quarter]
-    three[1] = inverse[half + quarter :, :quarter]
-    three[2] = inverse[half + quarter :, quarter:]
-    corner[...] = inverse[half : half + quarter, quarter:]
-
-    def load(tile, rows, start, size):
-        side = left if start < half else right
-        return side[tile, rows, start % half : start % half + size]
-
-    product(tiles, share, block, 1 - lax.axis_index("rows"), mask, load, high, low, out)
+    product(range(tiles), share, block, lax.axis_index("rows"), mask, load, high, low, out)
+
+
+def second_body(tile, share, block, mask, left, right, high, low, out):
+    half = left.shape[1]
+
+    def load(_, rows, start, size):
+        return left[rows, start : start + size] if start < half else right[tile, rows, start - half : start - half + size]
+
+    product([tile], share, block, 1 - lax.axis_index("rows"), mask, load, high, low, out)
+
+
+def halves_body(factor, *refs):
+    *outs, semaphores = refs
+    half = factor.shape[3] // 2
+    sources = [factor.at[0, tile, :, :half] for tile in range(factor.shape[1])] + [factor.at[0, :, :, half:]]
+    copies = [
+        pltpu.make_async_copy(source, out, semaphores.at[number])
+        for number, (source, out) in enumerate(zip(sources, outs))
+    ]
+    for copy in copies:
+        copy.start()
+    for copy in copies:
+        copy.wait()
 
 
 def hop_body(tiles, share, distances, pair, level, *refs):
     count = len(distances)
-    chunks, outs = refs[: 2 * count], refs[2 * count :]
+    groups, outs = [refs[:count], refs[count : (1 + tiles) * count]], refs[(1 + tiles) * count :]
     mine, theirs = outs[:2]
     flip, zero = lax.axis_index("rows"), lax.axis_index("depth") == 0
     rhs = pair[...]
     for group in range(2):
-        block = jnp.concatenate([chunks[group * count + i][...] for i in range(count)], axis=0)
+        block = jnp.concatenate([chunk[...] for chunk in groups[group]], axis=0)
         outs[2 + 2 * group][...], outs[3 + 2 * group][...] = split(jnp.transpose(block))
         value = folded(*split(block), rhs)
         half_index = jnp.where(flip == 0, group, 1 - group)
@@ -166,18 +173,26 @@
     out[...] = jnp.transpose(both[:shots] + both[shots:])
 
 
-def square_body(inverse, three, corner, near_high, near_low, far_high, far_low):
+def near_body(inverse, three, corner, near_high, near_low, turned_high, turned_low):
     half = inverse.shape[1]
+    quarter = half // 2
+    three[0] = inverse[half : half + quarter, :quarter]
+    three[1] = inverse[half + quarter :, :quarter]
+    three[2] = inverse[half + quarter :, quarter:]
+    corner[...] = inverse[half : half + quarter, quarter:]
     high, low = split(inverse[...])
-    turned_high, turned_low = jnp.transpose(high), jnp.transpose(low)
-    near = mm(turned_high, high) + mm(turned_high, low) + mm(turned_low, high)
+    left_high, left_low = jnp.transpose(high), jnp.transpose(low)
+    near = mm(left_high, high) + mm(left_high, low) + mm(left_low, high)
     near_high[...], near_low[...] = split(near)
+    turned_high[...], turned_low[...] = left_high[:, half:], left_low[:, half:]
+
+
+def far_body(turned_high, turned_low, three, corner, far_high, far_low):
     other = jnp.concatenate(
         [jnp.concatenate([three[0], corner[...]], axis=1), jnp.concatenate([three[1], three[2]], axis=1)], axis=0
     )
-    other_high, other_low = split(other)
-    turned_high, turned_low = turned_high[:, half:], turned_low[:, half:]
-    far = mm(turned_high, other_high) + mm(turned_high, other_low) + mm(turned_low, other_high)
+    high, low = split(other)
+    far = mm(turned_high[...], high) + mm(turned_high[...], low) + mm(turned_low[...], high)
     far_high[...], far_low[...] = split(far)
 
 
@@ -195,7 +210,7 @@
     )
 
 
-def couple(tiles, share, stages, start, mine, peer, flats, both):
+def couple(tiles, share, stages, start, mine, peer, flats, both, store, pieces):
     depth = lax.axis_index("depth")
     both[depth] = mine[...]
     both[1 - depth] = peer[...]
@@ -205,25 +220,44 @@
         )
         for distances in stages
     ]
-    highs, lows = [flat[...] for flat in flats[::2]], [flat[...] for flat in flats[1::2]]
-    if all(flat.shape[1] % 128 == 0 for flat in highs):
-        rows = [jnp.concatenate(rows, axis=0)]
-        highs, lows = [jnp.concatenate(highs, axis=1)], [jnp.concatenate(lows, axis=1)]
-    total = start[...]
-    for high, low, row in zip(highs, lows, rows):
-        total = total - folded(high, low, beside(row))
-    return total
+    size = start.shape[0] // pieces
+    joined = all(flat.shape[1] % 128 == 0 for flat in flats)
+    rights = [beside(jnp.concatenate(rows, axis=0))] if joined else [beside(row) for row in rows]
+    for piece in range(pieces):
+        at = slice(piece * size, (piece + 1) * size)
+        highs, lows = [flat[at, :] for flat in flats[::2]], [flat[at, :] for flat in flats[1::2]]
+        if joined:
+            highs, lows = [jnp.concatenate(highs, axis=1)], [jnp.concatenate(lows, axis=1)]
+        total = start[at, :]
+        for high, low, right in zip(highs, lows, rights):
+            total = total - folded(high, low, right)
+        store(piece, at, total)
 
 
 def couple_body(tiles, share, stages, start, mine, peer, *refs):
-    *flats, out, both = refs
-    out[...] = couple(tiles, share, stages, start, mine, peer, flats, both)
-
-
-def final_body(tiles, share, stages, start, mine, peer, top, *refs):
-    *flats, out, both = refs
-    out[0, 1] = top[...]
-    out[0, 0] = couple(tiles, share, stages, start, mine, peer, flats, both)
+    *flats, out, answer, both, semaphore = refs
+    copy = pltpu.make_async_copy(mine, answer.at[0, 1], semaphore)
+    copy.start()
+
+    def store(piece, at, total):
+        out[at, :] = total
+
+    couple(tiles, share, stages, start, mine, peer, flats, both, store, 1)
+    copy.wait()
+
+
+def final_body(tiles, share, stages, pieces, start, mine, peer, *refs):
+    *flats, _, answer, both, held, semaphores = refs
+    copies = []
+
+    def store(piece, at, total):
+        held[at, :] = total
+        copies.append(pltpu.make_async_copy(held.at[at, :], answer.at[0, 0, at, :], semaphores.at[piece]))
+        copies[-1].start()
+
+    couple(tiles, share, stages, start, mine, peer, flats, both, store, pieces)
+    for copy in copies:
+        copy.wait()
 
 
 def snake(count):
@@ -246,39 +280,52 @@
     shots = sources.shape[3]
     quarter = half // 2
 
-    far_right = lax.ppermute(factor[0, :, :, half:], "rows", swap)
-    far_left = lax.ppermute(factor[0, :, :, :half], "rows", [(1, 0)])
-    heavy = 8 * tiles * share * width * half
-    chunk = ((tiles * share, half), F32)
+    hold = pltpu.with_memory_space_constraint(factor, pltpu.HBM)
+    *lefts, right = call(
+        halves_body,
+        [((share, half), F32)] * tiles + [((tiles, share, half), F32)],
+        [hold],
+        0,
+        scratch=[pltpu.SemaphoreType.DMA((tiles + 1,))],
+        plain=(0,),
+    )
+    far_right = lax.ppermute(right, "rows", swap)
+    far_lefts = [lax.ppermute(left, "rows", [(1, 0)]) for left in lefts]
+    heavy = 8 * share * width * half
     own, high0, low0, pair0 = call(
         functools.partial(first_body, tiles, share, block),
-        [chunk] + [((width, half), BF16)] * 2 + [((half, 2 * shots), BF16)],
-        [block_mask, part_of(factor, 0), part_of(inverse_diagonal, 0, 0), part_of(sources, 0, 0)],
-        heavy,
-    )
-    far, three1, corner1 = call(
-        functools.partial(second_body, tiles, share, block),
-        [chunk, ((3, quarter, quarter), F32), ((quarter, quarter), F32)],
-        [block_mask, far_left, far_right, high0, low0, part_of(inverse_diagonal, 0, 1)],
-        heavy,
-    )
+        [((tiles * share, half), F32)] + [((width, half), BF16)] * 2 + [((half, 2 * shots), BF16)],
+        [part_of(block_mask, 0), part_of(factor, 0), part_of(inverse_diagonal, 0, 0), part_of(sources, 0, 0)],
+        heavy * tiles,
+    )
+    chains = [own]
+    for tile in range(tiles):
+        chains += call(
+            functools.partial(second_body, tile, share, block),
+            [((share, half), F32)],
+            [part_of(block_mask, 0), far_lefts[tile], far_right, high0, low0],
+            heavy,
+        )
 
     hops = shots_count // 2
-    stages, pieces = [[0]], [[[own], [far]]]
-    forward, backward = [own, far], [own, far]
+    stages, pieces = [[0]], [[[piece] for piece in chains]]
+    forward, backward = list(chains), list(chains)
     for hop in range(1, hops):
-        for number in range(2):
+        for number in range(len(chains)):
             forward[number] = lax.ppermute(forward[number], "shots", ahead)
             backward[number] = lax.ppermute(backward[number], "shots", behind)
         if hop == 1:
             stages[0] += [-1, 1]
-            for number in range(2):
+            for number in range(len(chains)):
                 pieces[0][number] += [forward[number], backward[number]]
         else:
             stages.append([-hop, hop])
             pieces.append([list(pair) for pair in zip(forward, backward)])
     stages.append([hops])
-    pieces.append([[lax.ppermute(forward[0], "shots", ahead)], [lax.ppermute(backward[1], "shots", behind)]])
+    pieces.append(
+        [[lax.ppermute(forward[0], "shots", ahead)]]
+        + [[lax.ppermute(backward[number], "shots", behind)] for number in range(1, len(chains))]
+    )
 
     part0, lower0 = call(
         start_body, [((width, shots), F32), ((half, shots), F32)], [high0, low0, pair0], 8 * width * half * shots
@@ -286,11 +333,17 @@
     far0 = lax.ppermute(lower0, "rows", swap)
     (base0,) = call(base_body, [((half, shots), F32)], [high0, low0, part0, far0], 8 * width * half * shots)
 
-    squares = call(
-        square_body,
-        [((half, half), BF16)] * 4,
-        [part_of(inverse_diagonal, 0, 1), lax.ppermute(three1, "rows", swap), lax.ppermute(corner1, "rows", [(0, 1)])],
-        9 * half * half * half * 2,
+    three1, corner1, *squares = call(
+        near_body,
+        [((3, quarter, quarter), F32), ((quarter, quarter), F32)] + [((half, half), BF16)] * 4,
+        [part_of(inverse_diagonal, 0, 1)],
+        6 * half * half * width,
+    )
+    squares[2:] = call(
+        far_body,
+        [((half, half), BF16)] * 2,
+        [*squares[2:], lax.ppermute(three1, "rows", swap), lax.ppermute(corner1, "rows", [(0, 1)])],
+        6 * half * half * half,
     )
 
     sums, others, flats = [], [], [[], []]
@@ -300,7 +353,9 @@
         mine, theirs, *flat = call(
             functools.partial(hop_body, tiles, share, distances),
             [((2 * count * share, shots), F32)] * 2 + [((half, deep), BF16)] * 4,
-            [pair0, part_of(sources, 0, 1)] + piece[0] + piece[1],
+            [pair0, part_of(sources, 0, 1)]
+            + piece[0]
+            + [chunk for row in zip(*piece[1:]) for chunk in row],
             16 * deep * half * shots,
         )
         total = mine + lax.ppermute(theirs, "depth", swap)
@@ -320,19 +375,30 @@
     peer_top = lax.ppermute(top, "depth", swap)
     peer_far = lax.ppermute(far_top, "depth", swap)
     work = 8 * half * width * shots
-    (almost,) = call(
+    shape = ((1, 2, half, shots), F32)
+    almost, answer = call(
         functools.partial(couple_body, tiles, share, stages),
-        [((half, shots), F32)],
+        [((half, shots), F32), shape],
         [base0, top, peer_top, *flats[0]],
         work,
-        scratch=[pltpu.VMEM((2, half, shots), F32)],
-    )
+        scratch=[pltpu.VMEM((2, half, shots), F32), pltpu.SemaphoreType.DMA],
+        placed=(1,),
+    )
+    pieces = 4 if half % 512 == 0 else 1
+    ins = [almost, far_top, peer_far, *flats[1], answer]
     (answer,) = call(
-        functools.partial(final_body, tiles, share, stages),
-        [((1, 2, half, shots), F32)],
-        [almost, far_top, peer_far, top, *flats[1]],
+        functools.partial(final_body, tiles, share, stages, pieces),
+        [shape],
+        ins,
         work,
-        scratch=[pltpu.VMEM((2, half, shots), F32)],
+        scratch=[
+            pltpu.VMEM((2, half, shots), F32),
+            pltpu.VMEM((half, shots), F32),
+            pltpu.SemaphoreType.DMA((pieces,)),
+        ],
+        plain=(len(ins) - 1,),
+        placed=(0,),
+        alias={len(ins) - 1: 0},
     )
     return answer
 

time: 94.3 us -> 98.7 us (1.047)
  Pallas kernels: 12.9 us -> 21.4 us
  local copies, waits for them, and re-layouts: 6.04 us -> 0 us
  starting transfers between devices: 35.4 us -> 41.1 us
  waiting for transfers between devices: 39.4 us -> 35.4 us
    ppermute x6 -> x9, waiting for transfers between devices: 18.4 us -> 6.08 us  [per_device(): backward[number] = lax.ppermute(backward[number], 'shots', behind)]
    pallas_call x12 -> x15, Pallas kernels: 12.9 us -> 21.4 us  [call(): pl.pallas_call(run, out_shape=[jax.ShapeDtypeStruct(shape, kind) for shap...]
    ppermute x6 -> x9, starting transfers between devices: 5.5 us -> 13.9 us  [per_device(): forward[number] = lax.ppermute(forward[number], 'shots', ahead)]
    ppermute x6 -> x9, waiting for transfers between devices: 0.02 us -> 6.84 us  [per_device(): forward[number] = lax.ppermute(forward[number], 'shots', ahead)]
    unnamed x12 -> x0, local copies, waits for them, and re-layouts: 4.98 us -> none
    ppermute x6 -> x9, starting transfers between devices: 11.8 us -> 7.25 us  [per_device(): backward[number] = lax.ppermute(backward[number], 'shots', behind)]
    ppermute x3 -> x5, starting transfers between devices: 6.3 us -> 8.76 us  [the longest x2 3.15 us: per_device(): lax.ppermute(backward[number], 'shots', behind)]
    ppermute x1, starting transfers between devices: 2.54 us -> 0.35 us  [per_device(): far_top = lax.ppermute(top, 'rows', swap)]
  transfers between devices with their start and end apart: 30 -> 38, of which waited for: 15 -> 15; matrix products, arithmetic and copies ran while one was open for 0% -> 0% of each run, Pallas kernels for 11% -> 18%
where the time goes in v1:
time: 98.7 us; the launch traced here: 98.2 us
  starting transfers between devices  41.1 us (42%)
  waiting for transfers between devices  35.4 us (36%)
  Pallas kernels  21.4 us (22%)
    pallas_call x15, Pallas kernels, call(): pl.pallas_call(run, out_shape=[jax.ShapeDtypeStruct(shape, kind) for shap...  21.4 us
    ppermute x9, starting transfers between devices, per_device(): forward[number] = lax.ppermute(forward[number], 'shots', ahead)  13.9 us
    ppermute x9, starting transfers between devices, per_device(): backward[number] = lax.ppermute(backward[number], 'shots', behind)  7.25 us
    ppermute x4, waiting for transfers between devices, per_device(): others.append(lax.ppermute(total, 'rows', swap))  7.12 us
    ppermute x9, waiting for transfers between devices, per_device(): forward[number] = lax.ppermute(forward[number], 'shots', ahead)  6.84 us
    ppermute x1, waiting for transfers between devices, per_device(): far_top = lax.ppermute(top, 'rows', swap)  6.38 us
    ppermute x9, waiting for transfers between devices, per_device(): backward[number] = lax.ppermute(backward[number], 'shots', behind)  6.08 us
    ppermute x2, waiting for transfers between devices, per_device(): far_lefts = [lax.ppermute(left, 'rows', [(1, 0)]) for left in lefts]  5.09 us
  transfers between devices with their start and end apart: 38, of which 15 were waited for; matrix products, arithmetic and copies ran while one was open for 0% of the time, Pallas kernels for 18%

profile of v1, /device:TPU:0, one launch (start us, length us, event | category | flops | bytes accessed | tf_op | source)
XLA Modules:
  0.0 98.2 jit_solution(1117146592781928211)
XLA Ops:
  1.1 3.0 %collective-permute-start.6 = (f32[2,64,512]{2,1,0:T(8,128)S(1)}, f32[2,64,512]{2,1,0:T(8,128)S(1)}, u32[]{:S(2)}, u32[]{:S(2)}) collective-permute-start(f32[2,64,512]{2,1,0:T(8,128)S(1)} %get-tuple-element.63), channel_id=1, source_target_pairs={{0,8},{8,0},{1,9},{9,1},{2,10},{10,2},{3,11},{11,3},{4,12},{12,4},... | collective-permute-start | bytes 786440 | tf_op jit(solution)/shard_map/ppermute | solution.py:292
  4.1 2.7 %shard_map.46 = (f32[128,512]{1,0:T(8,128)S(1)}, bf16[1024,512]{1,0:T(8,128)(2,1)S(1)}, bf16[1024,512]{1,0:T(8,128)(2,1)S(1)}, bf16[512,256]{1,0:T(8,128)(2,1)S(1)}) custom-call(s32[1,2,8,8]{3,2,1,0:T(8,128)} %refs_0_.9, f32[1,2,64,1024]{3,2,1,0:T(8,128)} %refs_0_.7, f32[1,2,1024,512]{3,2,1,0:T(8,128)} %refs_0_.6, f32[1,2,512,128]{3,2,1,0:T(8,128)} %refs_1_.9), custom_call_target="tpu_custom_call" | custom-call | flops 536870912 | bytes 5243392 | tf_op jit(solution)/shard_map/pallas_call | solution.py:67
  6.8 1.6 %collective-permute-start.3 = (f32[128,512]{1,0:T(8,128)S(1)}, f32[128,512]{1,0:T(8,128)S(1)}, u32[]{:S(2)}, u32[]{:S(2)}) collective-permute-start(f32[128,512]{1,0:T(8,128)S(1)} %get-tuple-element.61.refs_2_), channel_id=1, source_target_pairs={{0,2},{2,4},{4,6},{6,7},{7,5},{5,3},{3,1},{1,0},{8,10},{10,12},{12... | collective-permute-start | bytes 786440 | tf_op jit(solution)/shard_map/ppermute | solution.py:315
  10.2 1.3 %collective-permute-start.7 = (f32[64,512]{1,0:T(8,128)S(1)}, f32[64,512]{1,0:T(8,128)S(1)}, u32[]{:S(2)}, u32[]{:S(2)}) collective-permute-start(f32[64,512]{1,0:T(8,128)S(1)} %get-tuple-element.64), channel_id=1, source_target_pairs={{8,0},{9,1},{10,2},{11,3},{12,4},{13,5},{14,6},{15,7},{24,16},{25,... | collective-permute-start | bytes 393224 | tf_op jit(solution)/shard_map/ppermute | solution.py:293
  11.5 5.1 %collective-permute-done.5.refs_1_ = f32[64,512]{1,0:T(8,128)S(1)} collective-permute-done((f32[64,512]{1,0:T(8,128)S(1)}, f32[64,512]{1,0:T(8,128)S(1)}, u32[]{:S(2)}, u32[]{:S(2)}) %collective-permute-start.5) | collective-permute-done | bytes 131104 | tf_op jit(solution)/shard_map/ppermute | solution.py:293
  17.8 1.6 %collective-permute-start.8 = (f32[64,512]{1,0:T(8,128)S(1)}, f32[64,512]{1,0:T(8,128)S(1)}, u32[]{:S(2)}, u32[]{:S(2)}) collective-permute-start(f32[64,512]{1,0:T(8,128)S(1)} %shard_map.52.refs_5_), channel_id=1, source_target_pairs={{0,2},{2,4},{4,6},{6,7},{7,5},{5,3},{3,1},{1,0},{8,10},{10,12},{12... | collective-permute-start | bytes 393224 | tf_op jit(solution)/shard_map/ppermute | solution.py:315
  20.7 1.6 %collective-permute-start.9 = (f32[64,512]{1,0:T(8,128)S(1)}, f32[64,512]{1,0:T(8,128)S(1)}, u32[]{:S(2)}, u32[]{:S(2)}) collective-permute-start(f32[64,512]{1,0:T(8,128)S(1)} %shard_map.53.refs_6_), channel_id=1, source_target_pairs={{0,2},{2,4},{4,6},{6,7},{7,5},{5,3},{3,1},{1,0},{8,10},{10,12},{12... | collective-permute-start | bytes 393224 | tf_op jit(solution)/shard_map/ppermute | solution.py:315
  22.8 1.6 %collective-permute-start.13 = (f32[128,512]{1,0:T(8,128)S(1)}, f32[128,512]{1,0:T(8,128)S(1)}, u32[]{:S(2)}, u32[]{:S(2)}) collective-permute-start(f32[128,512]{1,0:T(8,128)S(1)} %collective-permute-done.3.refs_3_), channel_id=1, source_target_pairs={{0,2},{2,4},{4,6},{6,7},{7,5},{5,3},{3,1},{1,0},{8,10},{10,12},{12... | collective-permute-start | bytes 786440 | tf_op jit(solution)/shard_map/ppermute | solution.py:315
  25.8 1.4 %collective-permute-done.9.refs_8_ = f32[64,512]{1,0:T(8,128)S(1)} collective-permute-done((f32[64,512]{1,0:T(8,128)S(1)}, f32[64,512]{1,0:T(8,128)S(1)}, u32[]{:S(2)}, u32[]{:S(2)}) %collective-permute-start.9) | collective-permute-done | bytes 131104 | tf_op jit(solution)/shard_map/ppermute | solution.py:315
  27.1 1.6 %collective-permute-start.15 = (f32[64,512]{1,0:T(8,128)S(1)}, f32[64,512]{1,0:T(8,128)S(1)}, u32[]{:S(2)}, u32[]{:S(2)}) collective-permute-start(f32[64,512]{1,0:T(8,128)S(1)} %collective-permute-done.8.refs_7_), channel_id=1, source_target_pairs={{0,2},{2,4},{4,6},{6,7},{7,5},{5,3},{3,1},{1,0},{8,10},{10,12},{12... | collective-permute-start | bytes 393224 | tf_op jit(solution)/shard_map/ppermute | solution.py:315
  28.7 1.6 %collective-permute-start.16 = (f32[64,512]{1,0:T(8,128)S(1)}, f32[64,512]{1,0:T(8,128)S(1)}, u32[]{:S(2)}, u32[]{:S(2)}) collective-permute-start(f32[64,512]{1,0:T(8,128)S(1)} %collective-permute-done.9.refs_8_), channel_id=1, source_target_pairs={{0,2},{2,4},{4,6},{6,7},{7,5},{5,3},{3,1},{1,0},{8,10},{10,12},{12... | collective-permute-start | bytes 393224 | tf_op jit(solution)/shard_map/ppermute | solution.py:315
  30.3 3.5 %shard_map.49 = (f32[3,256,256]{2,1,0:T(8,128)S(1)}, f32[256,256]{1,0:T(8,128)S(1)}, bf16[512,512]{1,0:T(8,128)(2,1)S(1)}, bf16[512,512]{1,0:T(8,128)(2,1)S(1)},...) custom-call(f32[1,2,1024,512]{3,2,1,0:T(8,128)} %refs_0_.6), custom_call_target="tpu_custom_call" | custom-call | flops 1610612736 | bytes 4194304 | tf_op jit(solution)/shard_map/pallas_call | solution.py:67
  34.9 1.6 %shard_map.54 = (f32[384,128]{1,0:T(8,128)S(1)}, f32[384,128]{1,0:T(8,128)S(1)}, bf16[512,384]{1,0:T(8,128)(2,1)S(1)}, bf16[512,384]{1,0:T(8,128)(2,1)S(1)}, bf1...) custom-call(bf16[512,256]{1,0:T(8,128)(2,1)S(1)} %get-tuple-element.50.refs_2_.refs_0_, ...), custom_call_target="tpu_custom_call" | custom-call | flops 402653184 | bytes 2359296 | tf_op jit(solution)/shard_map/pallas_call | solution.py:67
  39.4 1.6 %collective-permute-start.22 = (f32[64,512]{1,0:T(8,128)S(1)}, f32[64,512]{1,0:T(8,128)S(1)}, u32[]{:S(2)}, u32[]{:S(2)}) collective-permute-start(f32[64,512]{1,0:T(8,128)S(1)} %collective-permute-done.15.refs_4_), channel_id=1, source_target_pairs={{0,2},{2,4},{4,6},{6,7},{7,5},{5,3},{3,1},{1,0},{8,10},{10,12},{12... | collective-permute-start | bytes 393224 | tf_op jit(solution)/shard_map/ppermute | solution.py:315
  41.0 1.5 %collective-permute-done.18.refs_7_ = f32[64,512]{1,0:T(8,128)S(1)} collective-permute-done((f32[64,512]{1,0:T(8,128)S(1)}, f32[64,512]{1,0:T(8,128)S(1)}, u32[]{:S(2)}, u32[]{:S(2)}) %collective-permute-start.18) | collective-permute-done | bytes 131104 | tf_op jit(solution)/shard_map/ppermute | solution.py:316
  42.5 1.6 %collective-permute-start.23 = (f32[64,512]{1,0:T(8,128)S(1)}, f32[64,512]{1,0:T(8,128)S(1)}, u32[]{:S(2)}, u32[]{:S(2)}) collective-permute-start(f32[64,512]{1,0:T(8,128)S(1)} %collective-permute-done.16.refs_5_), channel_id=1, source_target_pairs={{0,2},{2,4},{4,6},{6,7},{7,5},{5,3},{3,1},{1,0},{8,10},{10,12},{12... | collective-permute-start | bytes 393224 | tf_op jit(solution)/shard_map/ppermute | solution.py:315
  44.5 5.0 %collective-permute-done.22.refs_4_ = f32[64,512]{1,0:T(8,128)S(1)} collective-permute-done((f32[64,512]{1,0:T(8,128)S(1)}, f32[64,512]{1,0:T(8,128)S(1)}, u32[]{:S(2)}, u32[]{:S(2)}) %collective-permute-start.22) | collective-permute-done | bytes 131104 | tf_op jit(solution)/shard_map/ppermute | solution.py:315
  49.5 1.6 %collective-permute-start.24 = (f32[64,512]{1,0:T(8,128)S(1)}, f32[64,512]{1,0:T(8,128)S(1)}, u32[]{:S(2)}, u32[]{:S(2)}) collective-permute-start(f32[64,512]{1,0:T(8,128)S(1)} %collective-permute-done.17.refs_6_), channel_id=1, source_target_pairs={{2,0},{4,2},{6,4},{7,6},{5,7},{3,5},{1,3},{0,1},{10,8},{12,10},{14... | collective-permute-start | bytes 393224 | tf_op jit(solution)/shard_map/ppermute | solution.py:316
  51.5 1.6 %collective-permute-start.25 = (f32[64,512]{1,0:T(8,128)S(1)}, f32[64,512]{1,0:T(8,128)S(1)}, u32[]{:S(2)}, u32[]{:S(2)}) collective-permute-start(f32[64,512]{1,0:T(8,128)S(1)} %collective-permute-done.18.refs_7_), channel_id=1, source_target_pairs={{2,0},{4,2},{6,4},{7,6},{5,7},{3,5},{1,3},{0,1},{10,8},{12,10},{14... | collective-permute-start | bytes 393224 | tf_op jit(solution)/shard_map/ppermute | solution.py:316
  53.5 2.0 %collective-permute-done.24.refs_6_ = f32[64,512]{1,0:T(8,128)S(1)} collective-permute-done((f32[64,512]{1,0:T(8,128)S(1)}, f32[64,512]{1,0:T(8,128)S(1)}, u32[]{:S(2)}, u32[]{:S(2)}) %collective-permute-start.24) | collective-permute-done | bytes 131104 | tf_op jit(solution)/shard_map/ppermute | solution.py:316
  55.5 1.6 %collective-permute-start.28 = (f32[64,512]{1,0:T(8,128)S(1)}, f32[64,512]{1,0:T(8,128)S(1)}, u32[]{:S(2)}, u32[]{:S(2)}) collective-permute-start(f32[64,512]{1,0:T(8,128)S(1)} %collective-permute-done.24.refs_6_), channel_id=1, source_target_pairs={{2,0},{4,2},{6,4},{7,6},{5,7},{3,5},{1,3},{0,1},{10,8},{12,10},{14... | collective-permute-start | bytes 393224 | tf_op jit(solution)/shard_map/ppermute | solution.py:327
  58.3 1.6 %collective-permute-start.29 = (f32[64,512]{1,0:T(8,128)S(1)}, f32[64,512]{1,0:T(8,128)S(1)}, u32[]{:S(2)}, u32[]{:S(2)}) collective-permute-start(f32[64,512]{1,0:T(8,128)S(1)} %collective-permute-done.25.refs_7_), channel_id=1, source_target_pairs={{2,0},{4,2},{6,4},{7,6},{5,7},{3,5},{1,3},{0,1},{10,8},{12,10},{14... | collective-permute-start | bytes 393224 | tf_op jit(solution)/shard_map/ppermute | solution.py:327
  59.9 3.5 %collective-permute-start.2 = (f32[256,256]{1,0:T(8,128)S(1)}, f32[256,256]{1,0:T(8,128)S(1)}, u32[]{:S(2)}, u32[]{:S(2)}) collective-permute-start(f32[256,256]{1,0:T(8,128)S(1)} %get-tuple-element.58), channel_id=1, source_target_pairs={{0,8},{1,9},{2,10},{3,11},{4,12},{5,13},{6,14},{7,15},{16,24},{17,... | collective-permute-start | bytes 786440 | tf_op jit(solution)/shard_map/ppermute | solution.py:345
  63.4 1.4 %shard_map.55 = (f32[256,128]{1,0:T(8,128)S(1)}, f32[256,128]{1,0:T(8,128)S(1)}, bf16[512,256]{1,0:T(8,128)(2,1)S(1)}, bf16[512,256]{1,0:T(8,128)(2,1)S(1)}, bf1...) custom-call(bf16[512,256]{1,0:T(8,128)(2,1)S(1)} %get-tuple-element.50.refs_2_.refs_0_, ...), custom_call_target="tpu_custom_call" | custom-call | flops 268435456 | bytes 1835008 | tf_op jit(solution)/shard_map/pallas_call | solution.py:67
  64.9 1.4 %shard_map.56 = (f32[256,128]{1,0:T(8,128)S(1)}, f32[256,128]{1,0:T(8,128)S(1)}, bf16[512,256]{1,0:T(8,128)(2,1)S(1)}, bf16[512,256]{1,0:T(8,128)(2,1)S(1)}, bf1...) custom-call(bf16[512,256]{1,0:T(8,128)(2,1)S(1)} %get-tuple-element.50.refs_2_.refs_0_, ...), custom_call_target="tpu_custom_call" | custom-call | flops 268435456 | bytes 1835008 | tf_op jit(solution)/shard_map/pallas_call | solution.py:67
  68.5 2.1 %collective-permute-start.32 = (f32[256,128]{1,0:T(8,128)S(1)}, f32[256,128]{1,0:T(8,128)S(1)}, u32[]{:S(2)}, u32[]{:S(2)}) collective-permute-start(f32[256,128]{1,0:T(8,128)S(1)} %add.13.refs_5_), channel_id=1, source_target_pairs={{0,8},{8,0},{1,9},{9,1},{2,10},{10,2},{3,11},{11,3},{4,12},{12,4},... | collective-permute-start | bytes 393224 | tf_op jit(solution)/shard_map/ppermute | solution.py:363
  74.8 2.8 %collective-permute-done.32.refs_9_ = f32[256,128]{1,0:T(8,128)S(1)} collective-permute-done((f32[256,128]{1,0:T(8,128)S(1)}, f32[256,128]{1,0:T(8,128)S(1)}, u32[]{:S(2)}, u32[]{:S(2)}) %collective-permute-start.32) | collective-permute-done | bytes 131104 | tf_op jit(solution)/shard_map/ppermute | solution.py:363
  77.6 2.6 %collective-permute-done.33.refs_10_ = f32[256,128]{1,0:T(8,128)S(1)} collective-permute-done((f32[256,128]{1,0:T(8,128)S(1)}, f32[256,128]{1,0:T(8,128)S(1)}, u32[]{:S(2)}, u32[]{:S(2)}) %collective-permute-start.33) | collective-permute-done | bytes 131104 | tf_op jit(solution)/shard_map/ppermute | solution.py:363
  82.7 1.8 %collective-permute-start = (f32[512,128]{1,0:T(8,128)S(1)}, f32[512,128]{1,0:T(8,128)S(1)}, u32[]{:S(2)}, u32[]{:S(2)}) collective-permute-start(f32[512,128]{1,0:T(8,128)S(1)} %get-tuple-element.52), channel_id=1, source_target_pairs={{0,8},{8,0},{1,9},{9,1},{2,10},{10,2},{3,11},{11,3},{4,12},{12,4},... | collective-permute-start | bytes 786440 | tf_op jit(solution)/shard_map/ppermute | solution.py:333
  84.5 6.4 %collective-permute-done.36.refs_1_ = f32[512,128]{1,0:T(8,128)S(1)} collective-permute-done((f32[512,128]{1,0:T(8,128)S(1)}, f32[512,128]{1,0:T(8,128)S(1)}, u32[]{:S(2)}, u32[]{:S(2)}) %collective-permute-start.36) | collective-permute-done | bytes 262176 | tf_op jit(solution)/shard_map/ppermute | solution.py:374
  90.9 3.8 %collective-permute-done.refs_3_ = f32[512,128]{1,0:T(8,128)S(1)} collective-permute-done((f32[512,128]{1,0:T(8,128)S(1)}, f32[512,128]{1,0:T(8,128)S(1)}, u32[]{:S(2)}, u32[]{:S(2)}) %collective-permute-start) | collective-permute-done | bytes 262176 | tf_op jit(solution)/shard_map/ppermute | solution.py:333
  96.7 1.5 %shard_map.60 = f32[1,2,512,128]{3,2,1,0:T(8,128)} custom-call(f32[512,128]{1,0:T(8,128)S(1)} %get-tuple-element.81.refs_0_, f32[512,128]{1,0:T(8,128)S(1)} %collective-permute-done.36.refs_1_, f32[512,128]{1,0:T(8,128)S(1)} %collective-permute-done.37.refs_2_, bf16[512,384]{1,0:T(8,128)(2,1)S(1)} %get-tuple-element.82.refs_3_, ...), custom_call_target="tpu_custom_call", output_to_operand_aliasing={{}: (11, {})} | custom-call | flops 536870912 | bytes 3407872 | tf_op jit(solution)/shard_map/pallas_call | solution.py:67
  (63 shorter events, 24.5 us)
Async XLA Ops:
  1.1 15.5 %collective-permute-start.6 = (f32[2,64,512]{2,1,0:T(8,128)S(1)}, f32[2,64,512]{2,1,0:T(8,128)S(1)}, u32[]{:S(2)}, u32[]{:S(2)}) collective-permute-start(f32[2,64,512]{2,1,0:T(8,128)S(1)} %get-tuple-element.63), channel_id=1, source_target_pairs={{0,8},{8,0},{1,9},{9,1},{2,10},{10,2},{3,11},{11,3},{4,12},{12,4},... | collective-permute-start | bytes 786440 | tf_op jit(solution)/shard_map/ppermute | solution.py:292
  6.8 16.0 %collective-permute-start.3 = (f32[128,512]{1,0:T(8,128)S(1)}, f32[128,512]{1,0:T(8,128)S(1)}, u32[]{:S(2)}, u32[]{:S(2)}) collective-permute-start(f32[128,512]{1,0:T(8,128)S(1)} %get-tuple-element.61.refs_2_), channel_id=1, source_target_pairs={{0,2},{2,4},{4,6},{6,7},{7,5},{5,3},{3,1},{1,0},{8,10},{10,12},{12... | collective-permute-start | bytes 786440 | tf_op jit(solution)/shard_map/ppermute | solution.py:315
  8.5 15.9 %collective-permute-start.4 = (f32[128,512]{1,0:T(8,128)S(1)}, f32[128,512]{1,0:T(8,128)S(1)}, u32[]{:S(2)}, u32[]{:S(2)}) collective-permute-start(f32[128,512]{1,0:T(8,128)S(1)} %get-tuple-element.61.refs_2_), channel_id=1, source_target_pairs={{2,0},{4,2},{6,4},{7,6},{5,7},{3,5},{1,3},{0,1},{10,8},{12,10},{14... | collective-permute-start | bytes 786440 | tf_op jit(solution)/shard_map/ppermute | solution.py:316
  8.9 7.7 %collective-permute-start.5 = (f32[64,512]{1,0:T(8,128)S(1)}, f32[64,512]{1,0:T(8,128)S(1)}, u32[]{:S(2)}, u32[]{:S(2)}) collective-permute-start(f32[64,512]{1,0:T(8,128)S(1)} %get-tuple-element.62), channel_id=1, source_target_pairs={{8,0},{9,1},{10,2},{11,3},{12,4},{13,5},{14,6},{15,7},{24,16},{25,... | collective-permute-start | bytes 393224 | tf_op jit(solution)/shard_map/ppermute | solution.py:293
  10.2 9.3 %collective-permute-start.7 = (f32[64,512]{1,0:T(8,128)S(1)}, f32[64,512]{1,0:T(8,128)S(1)}, u32[]{:S(2)}, u32[]{:S(2)}) collective-permute-start(f32[64,512]{1,0:T(8,128)S(1)} %get-tuple-element.64), channel_id=1, source_target_pairs={{8,0},{9,1},{10,2},{11,3},{12,4},{13,5},{14,6},{15,7},{24,16},{25,... | collective-permute-start | bytes 393224 | tf_op jit(solution)/shard_map/ppermute | solution.py:293
  17.8 7.0 %collective-permute-start.8 = (f32[64,512]{1,0:T(8,128)S(1)}, f32[64,512]{1,0:T(8,128)S(1)}, u32[]{:S(2)}, u32[]{:S(2)}) collective-permute-start(f32[64,512]{1,0:T(8,128)S(1)} %shard_map.52.refs_5_), channel_id=1, source_target_pairs={{0,2},{2,4},{4,6},{6,7},{7,5},{5,3},{3,1},{1,0},{8,10},{10,12},{12... | collective-permute-start | bytes 393224 | tf_op jit(solution)/shard_map/ppermute | solution.py:315
  20.7 6.4 %collective-permute-start.9 = (f32[64,512]{1,0:T(8,128)S(1)}, f32[64,512]{1,0:T(8,128)S(1)}, u32[]{:S(2)}, u32[]{:S(2)}) collective-permute-start(f32[64,512]{1,0:T(8,128)S(1)} %shard_map.53.refs_6_), channel_id=1, source_target_pairs={{0,2},{2,4},{4,6},{6,7},{7,5},{5,3},{3,1},{1,0},{8,10},{10,12},{12... | collective-permute-start | bytes 393224 | tf_op jit(solution)/shard_map/ppermute | solution.py:315
  22.4 6.4 %collective-permute-start.10 = (f32[64,512]{1,0:T(8,128)S(1)}, f32[64,512]{1,0:T(8,128)S(1)}, u32[]{:S(2)}, u32[]{:S(2)}) collective-permute-start(f32[64,512]{1,0:T(8,128)S(1)} %shard_map.52.refs_5_), channel_id=1, source_target_pairs={{2,0},{4,2},{6,4},{7,6},{5,7},{3,5},{1,3},{0,1},{10,8},{12,10},{14... | collective-permute-start | bytes 393224 | tf_op jit(solution)/shard_map/ppermute | solution.py:316
  22.8 11.6 %collective-permute-start.13 = (f32[128,512]{1,0:T(8,128)S(1)}, f32[128,512]{1,0:T(8,128)S(1)}, u32[]{:S(2)}, u32[]{:S(2)}) collective-permute-start(f32[128,512]{1,0:T(8,128)S(1)} %collective-permute-done.3.refs_3_), channel_id=1, source_target_pairs={{0,2},{2,4},{4,6},{6,7},{7,5},{5,3},{3,1},{1,0},{8,10},{10,12},{12... | collective-permute-start | bytes 786440 | tf_op jit(solution)/shard_map/ppermute | solution.py:315
  24.4 12.1 %collective-permute-start.14 = (f32[128,512]{1,0:T(8,128)S(1)}, f32[128,512]{1,0:T(8,128)S(1)}, u32[]{:S(2)}, u32[]{:S(2)}) collective-permute-start(f32[128,512]{1,0:T(8,128)S(1)} %collective-permute-done.4.refs_4_), channel_id=1, source_target_pairs={{2,0},{4,2},{6,4},{7,6},{5,7},{3,5},{1,3},{0,1},{10,8},{12,10},{14... | collective-permute-start | bytes 786440 | tf_op jit(solution)/shard_map/ppermute | solution.py:316
  24.8 9.6 %collective-permute-start.11 = (f32[64,512]{1,0:T(8,128)S(1)}, f32[64,512]{1,0:T(8,128)S(1)}, u32[]{:S(2)}, u32[]{:S(2)}) collective-permute-start(f32[64,512]{1,0:T(8,128)S(1)} %shard_map.53.refs_6_), channel_id=1, source_target_pairs={{2,0},{4,2},{6,4},{7,6},{5,7},{3,5},{1,3},{0,1},{10,8},{12,10},{14... | collective-permute-start | bytes 393224 | tf_op jit(solution)/shard_map/ppermute | solution.py:316
  27.1 9.4 %collective-permute-start.15 = (f32[64,512]{1,0:T(8,128)S(1)}, f32[64,512]{1,0:T(8,128)S(1)}, u32[]{:S(2)}, u32[]{:S(2)}) collective-permute-start(f32[64,512]{1,0:T(8,128)S(1)} %collective-permute-done.8.refs_7_), channel_id=1, source_target_pairs={{0,2},{2,4},{4,6},{6,7},{7,5},{5,3},{3,1},{1,0},{8,10},{10,12},{12... | collective-permute-start | bytes 393224 | tf_op jit(solution)/shard_map/ppermute | solution.py:315
  28.7 8.8 %collective-permute-start.16 = (f32[64,512]{1,0:T(8,128)S(1)}, f32[64,512]{1,0:T(8,128)S(1)}, u32[]{:S(2)}, u32[]{:S(2)}) collective-permute-start(f32[64,512]{1,0:T(8,128)S(1)} %collective-permute-done.9.refs_8_), channel_id=1, source_target_pairs={{0,2},{2,4},{4,6},{6,7},{7,5},{5,3},{3,1},{1,0},{8,10},{10,12},{12... | collective-permute-start | bytes 393224 | tf_op jit(solution)/shard_map/ppermute | solution.py:315
  34.4 38.3 %collective-permute-start.1 = (f32[3,256,256]{2,1,0:T(8,128)S(1)}, f32[3,256,256]{2,1,0:T(8,128)S(1)}, u32[]{:S(2)}, u32[]{:S(2)}) collective-permute-start(f32[3,256,256]{2,1,0:T(8,128)S(1)} %get-tuple-element.57), channel_id=1, source_target_pairs={{0,8},{8,0},{1,9},{9,1},{2,10},{10,2},{3,11},{11,3},{4,12},{12,4},... | collective-permute-start | bytes 2359304 | tf_op jit(solution)/shard_map/ppermute | solution.py:345
  36.5 7.6 %collective-permute-start.12 = (f32[384,128]{1,0:T(8,128)S(1)}, f32[384,128]{1,0:T(8,128)S(1)}, u32[]{:S(2)}, u32[]{:S(2)}) collective-permute-start(f32[384,128]{1,0:T(8,128)S(1)} %get-tuple-element.66), channel_id=1, source_target_pairs={{0,16},{16,0},{1,17},{17,1},{2,18},{18,2},{3,19},{19,3},{4,20},{20... | collective-permute-start | bytes 589832 | tf_op jit(solution)/shard_map/ppermute | solution.py:361
  37.5 15.6 %collective-permute-start.20 = (f32[128,512]{1,0:T(8,128)S(1)}, f32[128,512]{1,0:T(8,128)S(1)}, u32[]{:S(2)}, u32[]{:S(2)}) collective-permute-start(f32[128,512]{1,0:T(8,128)S(1)} %collective-permute-done.13.refs_2_), channel_id=1, source_target_pairs={{0,2},{2,4},{4,6},{6,7},{7,5},{5,3},{3,1},{1,0},{8,10},{10,12},{12... | collective-permute-start | bytes 786440 | tf_op jit(solution)/shard_map/ppermute | solution.py:315
  39.4 10.1 %collective-permute-start.22 = (f32[64,512]{1,0:T(8,128)S(1)}, f32[64,512]{1,0:T(8,128)S(1)}, u32[]{:S(2)}, u32[]{:S(2)}) collective-permute-start(f32[64,512]{1,0:T(8,128)S(1)} %collective-permute-done.15.refs_4_), channel_id=1, source_target_pairs={{0,2},{2,4},{4,6},{6,7},{7,5},{5,3},{3,1},{1,0},{8,10},{10,12},{12... | collective-permute-start | bytes 393224 | tf_op jit(solution)/shard_map/ppermute | solution.py:315
  42.5 9.0 %collective-permute-start.23 = (f32[64,512]{1,0:T(8,128)S(1)}, f32[64,512]{1,0:T(8,128)S(1)}, u32[]{:S(2)}, u32[]{:S(2)}) collective-permute-start(f32[64,512]{1,0:T(8,128)S(1)} %collective-permute-done.16.refs_5_), channel_id=1, source_target_pairs={{0,2},{2,4},{4,6},{6,7},{7,5},{5,3},{3,1},{1,0},{8,10},{10,12},{12... | collective-permute-start | bytes 393224 | tf_op jit(solution)/shard_map/ppermute | solution.py:315
  44.0 15.9 %collective-permute-start.21 = (f32[128,512]{1,0:T(8,128)S(1)}, f32[128,512]{1,0:T(8,128)S(1)}, u32[]{:S(2)}, u32[]{:S(2)}) collective-permute-start(f32[128,512]{1,0:T(8,128)S(1)} %collective-permute-done.14.refs_3_), channel_id=1, source_target_pairs={{2,0},{4,2},{6,4},{7,6},{5,7},{3,5},{1,3},{0,1},{10,8},{12,10},{14... | collective-permute-start | bytes 786440 | tf_op jit(solution)/shard_map/ppermute | solution.py:316
  49.5 6.0 %collective-permute-start.24 = (f32[64,512]{1,0:T(8,128)S(1)}, f32[64,512]{1,0:T(8,128)S(1)}, u32[]{:S(2)}, u32[]{:S(2)}) collective-permute-start(f32[64,512]{1,0:T(8,128)S(1)} %collective-permute-done.17.refs_6_), channel_id=1, source_target_pairs={{2,0},{4,2},{6,4},{7,6},{5,7},{3,5},{1,3},{0,1},{10,8},{12,10},{14... | collective-permute-start | bytes 393224 | tf_op jit(solution)/shard_map/ppermute | solution.py:316
  51.5 6.9 %collective-permute-start.25 = (f32[64,512]{1,0:T(8,128)S(1)}, f32[64,512]{1,0:T(8,128)S(1)}, u32[]{:S(2)}, u32[]{:S(2)}) collective-permute-start(f32[64,512]{1,0:T(8,128)S(1)} %collective-permute-done.18.refs_7_), channel_id=1, source_target_pairs={{2,0},{4,2},{6,4},{7,6},{5,7},{3,5},{1,3},{0,1},{10,8},{12,10},{14... | collective-permute-start | bytes 393224 | tf_op jit(solution)/shard_map/ppermute | solution.py:316
  53.1 13.9 %collective-permute-start.27 = (f32[128,512]{1,0:T(8,128)S(1)}, f32[128,512]{1,0:T(8,128)S(1)}, u32[]{:S(2)}, u32[]{:S(2)}) collective-permute-start(f32[128,512]{1,0:T(8,128)S(1)} %collective-permute-done.20.refs_2_), channel_id=1, source_target_pairs={{0,2},{2,4},{4,6},{6,7},{7,5},{5,3},{3,1},{1,0},{8,10},{10,12},{12... | collective-permute-start | bytes 786440 | tf_op jit(solution)/shard_map/ppermute | solution.py:326
  55.5 9.3 %collective-permute-start.28 = (f32[64,512]{1,0:T(8,128)S(1)}, f32[64,512]{1,0:T(8,128)S(1)}, u32[]{:S(2)}, u32[]{:S(2)}) collective-permute-start(f32[64,512]{1,0:T(8,128)S(1)} %collective-permute-done.24.refs_6_), channel_id=1, source_target_pairs={{2,0},{4,2},{6,4},{7,6},{5,7},{3,5},{1,3},{0,1},{10,8},{12,10},{14... | collective-permute-start | bytes 393224 | tf_op jit(solution)/shard_map/ppermute | solution.py:327
  58.3 8.0 %collective-permute-start.29 = (f32[64,512]{1,0:T(8,128)S(1)}, f32[64,512]{1,0:T(8,128)S(1)}, u32[]{:S(2)}, u32[]{:S(2)}) collective-permute-start(f32[64,512]{1,0:T(8,128)S(1)} %collective-permute-done.25.refs_7_), channel_id=1, source_target_pairs={{2,0},{4,2},{6,4},{7,6},{5,7},{3,5},{1,3},{0,1},{10,8},{12,10},{14... | collective-permute-start | bytes 393224 | tf_op jit(solution)/shard_map/ppermute | solution.py:327
  59.9 11.8 %collective-permute-start.2 = (f32[256,256]{1,0:T(8,128)S(1)}, f32[256,256]{1,0:T(8,128)S(1)}, u32[]{:S(2)}, u32[]{:S(2)}) collective-permute-start(f32[256,256]{1,0:T(8,128)S(1)} %get-tuple-element.58), channel_id=1, source_target_pairs={{0,8},{1,9},{2,10},{3,11},{4,12},{5,13},{6,14},{7,15},{16,24},{17,... | collective-permute-start | bytes 786440 | tf_op jit(solution)/shard_map/ppermute | solution.py:345
  67.0 7.8 %collective-permute-start.31 = (f32[384,128]{1,0:T(8,128)S(1)}, f32[384,128]{1,0:T(8,128)S(1)}, u32[]{:S(2)}, u32[]{:S(2)}) collective-permute-start(f32[384,128]{1,0:T(8,128)S(1)} %add.12.refs_4_), channel_id=1, source_target_pairs={{0,8},{8,0},{1,9},{9,1},{2,10},{10,2},{3,11},{11,3},{4,12},{12,4},... | collective-permute-start | bytes 589832 | tf_op jit(solution)/shard_map/ppermute | solution.py:363
  68.5 9.1 %collective-permute-start.32 = (f32[256,128]{1,0:T(8,128)S(1)}, f32[256,128]{1,0:T(8,128)S(1)}, u32[]{:S(2)}, u32[]{:S(2)}) collective-permute-start(f32[256,128]{1,0:T(8,128)S(1)} %add.13.refs_5_), channel_id=1, source_target_pairs={{0,8},{8,0},{1,9},{9,1},{2,10},{10,2},{3,11},{11,3},{4,12},{12,4},... | collective-permute-start | bytes 393224 | tf_op jit(solution)/shard_map/ppermute | solution.py:363
  70.6 9.6 %collective-permute-start.33 = (f32[256,128]{1,0:T(8,128)S(1)}, f32[256,128]{1,0:T(8,128)S(1)}, u32[]{:S(2)}, u32[]{:S(2)}) collective-permute-start(f32[256,128]{1,0:T(8,128)S(1)} %add.14.refs_6_), channel_id=1, source_target_pairs={{0,8},{8,0},{1,9},{9,1},{2,10},{10,2},{3,11},{11,3},{4,12},{12,4},... | collective-permute-start | bytes 393224 | tf_op jit(solution)/shard_map/ppermute | solution.py:363
  71.7 9.2 %collective-permute-start.34 = (f32[128,128]{1,0:T(8,128)S(1)}, f32[128,128]{1,0:T(8,128)S(1)}, u32[]{:S(2)}, u32[]{:S(2)}) collective-permute-start(f32[128,128]{1,0:T(8,128)S(1)} %add.15.refs_7_), channel_id=1, source_target_pairs={{0,8},{8,0},{1,9},{9,1},{2,10},{10,2},{3,11},{11,3},{4,12},{12,4},... | collective-permute-start | bytes 196616 | tf_op jit(solution)/shard_map/ppermute | solution.py:363
  81.7 9.2 %collective-permute-start.36 = (f32[512,128]{1,0:T(8,128)S(1)}, f32[512,128]{1,0:T(8,128)S(1)}, u32[]{:S(2)}, u32[]{:S(2)}) collective-permute-start(f32[512,128]{1,0:T(8,128)S(1)} %shard_map.58.refs_1_), channel_id=1, source_target_pairs={{0,8},{8,0},{1,9},{9,1},{2,10},{10,2},{3,11},{11,3},{4,12},{12,4},... | collective-permute-start | bytes 786440 | tf_op jit(solution)/shard_map/ppermute | solution.py:374
  82.7 12.0 %collective-permute-start = (f32[512,128]{1,0:T(8,128)S(1)}, f32[512,128]{1,0:T(8,128)S(1)}, u32[]{:S(2)}, u32[]{:S(2)}) collective-permute-start(f32[512,128]{1,0:T(8,128)S(1)} %get-tuple-element.52), channel_id=1, source_target_pairs={{0,8},{8,0},{1,9},{9,1},{2,10},{10,2},{3,11},{11,3},{4,12},{12,4},... | collective-permute-start | bytes 786440 | tf_op jit(solution)/shard_map/ppermute | solution.py:333
  84.5 11.1 %collective-permute-start.35 = (f32[512,128]{1,0:T(8,128)S(1)}, f32[512,128]{1,0:T(8,128)S(1)}, u32[]{:S(2)}, u32[]{:S(2)}) collective-permute-start(f32[512,128]{1,0:T(8,128)S(1)} %shard_map.58.refs_1_), channel_id=1, source_target_pairs={{0,16},{16,0},{1,17},{17,1},{2,18},{18,2},{3,19},{19,3},{4,20},{20... | collective-permute-start | bytes 786440 | tf_op jit(solution)/shard_map/ppermute | solution.py:375
  (6 other events, 24.4 us)

commit v2 on v1

--- a/solution.py
+++ b/solution.py
@@ -113,32 +113,65 @@
     product(range(tiles), share, block, lax.axis_index("rows"), mask, load, high, low, out)
 
 
-def second_body(tile, share, block, mask, left, right, high, low, out):
-    half = left.shape[1]
-
-    def load(_, rows, start, size):
-        return left[rows, start : start + size] if start < half else right[tile, rows, start - half : start - half + size]
-
-    product([tile], share, block, 1 - lax.axis_index("rows"), mask, load, high, low, out)
-
-
-def halves_body(factor, *refs):
-    *outs, semaphores = refs
-    half = factor.shape[3] // 2
-    sources = [factor.at[0, tile, :, :half] for tile in range(factor.shape[1])] + [factor.at[0, :, :, half:]]
-    copies = [
-        pltpu.make_async_copy(source, out, semaphores.at[number])
-        for number, (source, out) in enumerate(zip(sources, outs))
-    ]
-    for copy in copies:
-        copy.start()
-    for copy in copies:
-        copy.wait()
+def second_body(tiles, share, block, mask, received, high, low, out):
+    half = high.shape[1]
+    flip = lax.axis_index("rows")
+
+    def load(tile, rows, start, size):
+        if start >= half:
+            return received[tile, rows, start - half : start - half + size]
+        left = received[tile, share + rows.start : share + rows.stop, start : start + size]
+        return jnp.where(flip == 0, left, 0.0)
+
+    product(range(tiles), share, block, 1 - flip, mask, load, high, low, out)
+
+
+def halves_body(factor, inverse, out, semaphores):
+    tiles, share, width = factor.shape[1:]
+    half = width // 2
+    quarter, slab = half // 2, half // 8
+    flip = lax.axis_index("rows")
+
+    def copy(source, target, number):
+        return pltpu.make_async_copy(source, target, semaphores.at[number])
+
+    rights = [copy(factor.at[0, t, :, half:], out.at[t, :share, :], t) for t in range(tiles)]
+    for each in rights:
+        each.start()
+
+    @pl.when(flip == 1)
+    def _():
+        lefts = [copy(factor.at[0, t, :, :half], out.at[t, share : 2 * share, :], tiles + t) for t in range(tiles)]
+        for each in lefts:
+            each.start()
+        for each in lefts:
+            each.wait()
+
+    @pl.when(flip == 0)
+    def _():
+        corners = []
+        for t in range(tiles):
+            for side in range(2):
+                top = half + (2 * t + side) * slab
+                corners.append(
+                    copy(
+                        inverse.at[0, 1, top : top + slab, quarter:half],
+                        out.at[t, share : share + slab, side * quarter : (side + 1) * quarter],
+                        tiles + 2 * t + side,
+                    )
+                )
+        for each in corners:
+            each.start()
+        for each in corners:
+            each.wait()
+
+    for each in rights:
+        each.wait()
 
 
 def hop_body(tiles, share, distances, pair, level, *refs):
-    count = len(distances)
-    groups, outs = [refs[:count], refs[count : (1 + tiles) * count]], refs[(1 + tiles) * count :]
+    count, chunks = len(distances), (len(refs) - 6) // 2
+    groups, outs = [refs[:chunks], refs[chunks : 2 * chunks]], refs[2 * chunks :]
     mine, theirs = outs[:2]
     flip, zero = lax.axis_index("rows"), lax.axis_index("depth") == 0
     rhs = pair[...]
@@ -158,28 +191,45 @@
             theirs[at, :] = -jnp.where(zero, second, first)
 
 
-def start_body(high, low, pair, out, lower):
+def start_body(high, low, pair, inverse, sources, out, bulk, level, semaphores):
+    half = level.shape[0]
+    quarter, slab, shots = half // 2, half // 4, level.shape[1]
+
+    def copy(row, size, column, target, number):
+        source = inverse.at[0, 1, half + row : half + row + size, column : column + quarter]
+        return pltpu.make_async_copy(source, target, semaphores.at[number])
+
+    copies = [
+        copy(0, quarter, 0, bulk.at[:quarter, :quarter], 0),
+        copy(quarter, quarter, quarter, bulk.at[:quarter, quarter:], 1),
+        copy(quarter, slab, 0, bulk.at[quarter : quarter + slab, :quarter], 2),
+        copy(quarter + slab, slab, 0, bulk.at[quarter : quarter + slab, quarter:], 3),
+        pltpu.make_async_copy(sources.at[0, 1], level, semaphores.at[4]),
+    ]
+    for each in copies:
+        each.start()
     value = folded(high[...], low[...], pair[...])
     out[...] = value
-    lower[...] = value[value.shape[0] // 2 :]
-
-
-def base_body(high, low, part, far, out):
-    half = far.shape[0]
-    value = jnp.concatenate([part[:half, :], part[half:, :] + far[...]], axis=0)
-    rows = jnp.concatenate(split(jnp.transpose(value)), axis=0)
-    both = mm(rows, high[...]) + mm(rows, low[...])
-    shots = both.shape[0] // 2
+    for number in range(half // shots):
+        first = half + number * shots
+        bulk[quarter + slab :, number * shots : (number + 1) * shots] = value[first : first + shots]
+    for each in copies:
+        each.wait()
+
+
+def base_body(high, low, part, bulk, out):
+    half, shots = out.shape
+    far = jnp.concatenate(
+        [bulk[bulk.shape[0] - shots :, number * shots : (number + 1) * shots] for number in range(half // shots)], axis=0
+    )
+    value = jnp.concatenate([part[:half, :], part[half:, :] + far], axis=0)
+    stacked = jnp.concatenate(split(jnp.transpose(value)), axis=0)
+    both = mm(stacked, high[...]) + mm(stacked, low[...])
     out[...] = jnp.transpose(both[:shots] + both[shots:])
 
 
-def near_body(inverse, three, corner, near_high, near_low, turned_high, turned_low):
+def near_body(inverse, near_high, near_low, turned_high, turned_low):
     half = inverse.shape[1]
-    quarter = half // 2
-    three[0] = inverse[half : half + quarter, :quarter]
-    three[1] = inverse[half + quarter :, :quarter]
-    three[2] = inverse[half + quarter :, quarter:]
-    corner[...] = inverse[half : half + quarter, quarter:]
     high, low = split(inverse[...])
     left_high, left_low = jnp.transpose(high), jnp.transpose(low)
     near = mm(left_high, high) + mm(left_high, low) + mm(left_low, high)
@@ -187,9 +237,26 @@
     turned_high[...], turned_low[...] = left_high[:, half:], left_low[:, half:]
 
 
-def far_body(turned_high, turned_low, three, corner, far_high, far_low):
+def far_body(share, turned_high, turned_low, bulk, received, far_high, far_low):
+    half = bulk.shape[1]
+    quarter, slab = half // 2, half // 4
+    piece = slab // received.shape[0]
+    corner = jnp.concatenate(
+        [
+            received[t, share : share + piece, side * quarter : (side + 1) * quarter]
+            for t in range(received.shape[0])
+            for side in range(2)
+        ],
+        axis=0,
+    )
+    corner = jnp.where(lax.axis_index("rows") == 1, corner, 0.0)
+    bottom = jnp.concatenate([bulk[quarter : quarter + slab, :quarter], bulk[quarter : quarter + slab, quarter:]], axis=0)
     other = jnp.concatenate(
-        [jnp.concatenate([three[0], corner[...]], axis=1), jnp.concatenate([three[1], three[2]], axis=1)], axis=0
+        [
+            jnp.concatenate([bulk[:quarter, :quarter], corner], axis=1),
+            jnp.concatenate([bottom, bulk[:quarter, quarter:]], axis=1),
+        ],
+        axis=0,
     )
     high, low = split(other)
     far = mm(turned_high[...], high) + mm(turned_high[...], low) + mm(turned_low[...], high)
@@ -268,7 +335,8 @@
     shots_count = lax.axis_size("shots")
     rows_count = lax.axis_size("rows")
     depth_count = lax.axis_size("depth")
-    assert rows_count == 2 and depth_count == 2 and sources.shape[1] == 2 and shots_count % 2 == 0
+    assert rows_count == 2 and depth_count == 2 and sources.shape[1] == 2
+    assert shots_count % 2 == 0 and shots_count >= 4
     order = snake(shots_count)
     ahead = [(order[i], order[(i + 1) % shots_count]) for i in range(shots_count)]
     behind = [(b, a) for a, b in ahead]
@@ -280,69 +348,77 @@
     shots = sources.shape[3]
     quarter = half // 2
 
-    hold = pltpu.with_memory_space_constraint(factor, pltpu.HBM)
-    *lefts, right = call(
+    assert tiles == 2 and half % shots == 0
+    hold_factor, hold_inverse, hold_sources = (
+        pltpu.with_memory_space_constraint(x, pltpu.HBM) for x in (factor, inverse_diagonal, sources)
+    )
+    (halves,) = call(
         halves_body,
-        [((share, half), F32)] * tiles + [((tiles, share, half), F32)],
-        [hold],
+        [((tiles, share + max(share, half // 8), half), F32)],
+        [hold_factor, hold_inverse],
         0,
-        scratch=[pltpu.SemaphoreType.DMA((tiles + 1,))],
-        plain=(0,),
-    )
-    far_right = lax.ppermute(right, "rows", swap)
-    far_lefts = [lax.ppermute(left, "rows", [(1, 0)]) for left in lefts]
-    heavy = 8 * share * width * half
+        scratch=[pltpu.SemaphoreType.DMA((3 * tiles,))],
+        plain=(0, 1),
+    )
+    received = lax.ppermute(halves, "rows", swap)
+    heavy = 8 * tiles * share * width * half
     own, high0, low0, pair0 = call(
         functools.partial(first_body, tiles, share, block),
         [((tiles * share, half), F32)] + [((width, half), BF16)] * 2 + [((half, 2 * shots), BF16)],
         [part_of(block_mask, 0), part_of(factor, 0), part_of(inverse_diagonal, 0, 0), part_of(sources, 0, 0)],
-        heavy * tiles,
-    )
-    chains = [own]
-    for tile in range(tiles):
-        chains += call(
-            functools.partial(second_body, tile, share, block),
-            [((share, half), F32)],
-            [part_of(block_mask, 0), far_lefts[tile], far_right, high0, low0],
-            heavy,
-        )
+        heavy,
+    )
+    (far,) = call(
+        functools.partial(second_body, tiles, share, block),
+        [((tiles * share, half), F32)],
+        [part_of(block_mask, 0), received, high0, low0],
+        heavy,
+    )
 
     hops = shots_count // 2
-    stages, pieces = [[0]], [[[piece] for piece in chains]]
-    forward, backward = list(chains), list(chains)
+    stages, pieces = [[0]], [[[own], [far]]]
+    forward, backward = [own, far], [own, far]
     for hop in range(1, hops):
-        for number in range(len(chains)):
+        for number in range(2):
             forward[number] = lax.ppermute(forward[number], "shots", ahead)
             backward[number] = lax.ppermute(backward[number], "shots", behind)
-        if hop == 1:
-            stages[0] += [-1, 1]
-            for number in range(len(chains)):
+        if hop + 1 < hops:
+            stages[0] += [-hop, hop]
+            for number in range(2):
                 pieces[0][number] += [forward[number], backward[number]]
         else:
             stages.append([-hop, hop])
             pieces.append([list(pair) for pair in zip(forward, backward)])
     stages.append([hops])
     pieces.append(
-        [[lax.ppermute(forward[0], "shots", ahead)]]
-        + [[lax.ppermute(backward[number], "shots", behind)] for number in range(1, len(chains))]
-    )
-
-    part0, lower0 = call(
-        start_body, [((width, shots), F32), ((half, shots), F32)], [high0, low0, pair0], 8 * width * half * shots
-    )
-    far0 = lax.ppermute(lower0, "rows", swap)
-    (base0,) = call(base_body, [((half, shots), F32)], [high0, low0, part0, far0], 8 * width * half * shots)
-
-    three1, corner1, *squares = call(
-        near_body,
-        [((3, quarter, quarter), F32), ((quarter, quarter), F32)] + [((half, half), BF16)] * 4,
-        [part_of(inverse_diagonal, 0, 1)],
-        6 * half * half * width,
-    )
-    squares[2:] = call(
-        far_body,
+        [
+            [
+                lax.ppermute(forward[number][:share], "shots", ahead),
+                lax.ppermute(backward[number][share:], "shots", behind),
+            ]
+            for number in range(2)
+        ]
+    )
+
+    part0, bulk, level1 = call(
+        start_body,
+        [((width, shots), F32), ((quarter + half // 4 + shots, half), F32), ((half, shots), F32)],
+        [high0, low0, pair0, hold_inverse, hold_sources],
+        8 * width * half * shots,
+        scratch=[pltpu.SemaphoreType.DMA((5,))],
+        plain=(3, 4),
+    )
+    far_bulk = lax.ppermute(bulk, "rows", swap)
+    (base0,) = call(base_body, [((half, shots), F32)], [high0, low0, part0, far_bulk], 8 * width * half * shots)
+
+    near_high, near_low, *turned = call(
+        near_body, [((half, half), BF16)] * 4, [part_of(inverse_diagonal, 0, 1)], 6 * half * half * width
+    )
+    squares = [near_high, near_low]
+    squares += call(
+        functools.partial(far_body, share),
         [((half, half), BF16)] * 2,
-        [*squares[2:], lax.ppermute(three1, "rows", swap), lax.ppermute(corner1, "rows", [(0, 1)])],
+        [*turned, far_bulk, received],
         6 * half * half * half,
     )
 
@@ -353,9 +429,7 @@
         mine, theirs, *flat = call(
             functools.partial(hop_body, tiles, share, distances),
             [((2 * count * share, shots), F32)] * 2 + [((half, deep), BF16)] * 4,
-            [pair0, part_of(sources, 0, 1)]
-            + piece[0]
-            + [chunk for row in zip(*piece[1:]) for chunk in row],
+            [pair0, level1] + piece[0] + piece[1],
             16 * deep * half * shots,
         )
         total = mine + lax.ppermute(theirs, "depth", swap)

time: 98.7 us -> 81.9 us (0.83)
  starting transfers between devices: 41.1 us -> 29 us
  Pallas kernels: 21.4 us -> 16.9 us
    ppermute x9 -> x6, waiting for transfers between devices: 6.84 us -> 15.2 us  [per_device(): forward[number] = lax.ppermute(forward[number], 'shots', ahead)]
    ppermute x9 -> x6, starting transfers between devices: 14.5 us -> 8.86 us  [the longest x1 3.07 us: per_device(): received = lax.ppermute(halves, 'rows', swap)]
    ppermute x9 -> x6, waiting for transfers between devices: 6.08 us -> 1.06 us  [per_device(): backward[number] = lax.ppermute(backward[number], 'shots', behind)]
    pallas_call x15 -> x13, Pallas kernels: 21.4 us -> 16.9 us  [call(): pl.pallas_call(run, out_shape=[jax.ShapeDtypeStruct(shape, kind) for shap...]
    ppermute x4 -> x3, waiting for transfers between devices: 7.12 us -> 3.19 us  [per_device(): others.append(lax.ppermute(total, 'rows', swap))]
    ppermute x9 -> x6, starting transfers between devices: 7.25 us -> 3.34 us  [per_device(): backward[number] = lax.ppermute(backward[number], 'shots', behind)]
    ppermute x9 -> x6, starting transfers between devices: 13.9 us -> 10.6 us  [per_device(): forward[number] = lax.ppermute(forward[number], 'shots', ahead)]
    ppermute x1, starting transfers between devices: 0.35 us -> 1.81 us  [per_device(): far_top = lax.ppermute(top, 'rows', swap)]
  transfers between devices with their start and end apart: 38 -> 27, of which waited for: 15 -> 12; matrix products, arithmetic and copies ran while one was open for 0% -> 0% of each run, Pallas kernels for 18% -> 17%
where the time goes in v2:
time: 81.9 us; the launch traced here: 81.6 us
  waiting for transfers between devices  35.3 us (43%)
  starting transfers between devices  29 us (35%)
  Pallas kernels  16.9 us (21%)
    pallas_call x13, Pallas kernels, call(): pl.pallas_call(run, out_shape=[jax.ShapeDtypeStruct(shape, kind) for shap...  16.9 us
    ppermute x6, waiting for transfers between devices, per_device(): forward[number] = lax.ppermute(forward[number], 'shots', ahead)  15.2 us
    ppermute x6, starting transfers between devices, per_device(): forward[number] = lax.ppermute(forward[number], 'shots', ahead)  10.6 us
    ppermute x1, waiting for transfers between devices, per_device(): received = lax.ppermute(halves, 'rows', swap)  7.17 us
    ppermute x1, waiting for transfers between devices, per_device(): far_top = lax.ppermute(top, 'rows', swap)  6.32 us
    ppermute x3, starting transfers between devices, per_device(): others.append(lax.ppermute(total, 'rows', swap))  4.18 us
    ppermute x6, starting transfers between devices, per_device(): backward[number] = lax.ppermute(backward[number], 'shots', behind)  3.34 us
    ppermute x3, waiting for transfers between devices, per_device(): others.append(lax.ppermute(total, 'rows', swap))  3.19 us
  transfers between devices with their start and end apart: 27, of which 12 were waited for; matrix products, arithmetic and copies ran while one was open for 0% of the time, Pallas kernels for 17%

profile of v2, /device:TPU:0, one launch (start us, length us, event | category | flops | bytes accessed | tf_op | source)
XLA Modules:
  0.0 81.6 jit_solution(11855834267634962262)
XLA Ops:
  0.0 1.1 %shard_map.50 = f32[2,128,512]{2,1,0:T(8,128)S(1)} custom-call(f32[1,2,64,1024]{3,2,1,0:T(8,128)} %refs_0_.6, f32[1,2,1024,512]{3,2,1,0:T(8,128)} %refs_1_.3), custom_call_target="tpu_custom_call" | custom-call | bytes 4718592 | tf_op jit(solution)/shard_map/pallas_call | solution.py:67
  1.1 3.1 %collective-permute-start.1 = (f32[2,128,512]{2,1,0:T(8,128)S(1)}, f32[2,128,512]{2,1,0:T(8,128)S(1)}, u32[]{:S(2)}, u32[]{:S(2)}) collective-permute-start(f32[2,128,512]{2,1,0:T(8,128)S(1)} %shard_map.50), channel_id=1, source_target_pairs={{0,8},{8,0},{1,9},{9,1},{2,10},{10,2},{3,11},{11,3},{4,12},{12,4},... | collective-permute-start | bytes 1572872 | tf_op jit(solution)/shard_map/ppermute | solution.py:363
  4.2 2.7 %shard_map.46 = (f32[128,512]{1,0:T(8,128)S(1)}, bf16[1024,512]{1,0:T(8,128)(2,1)S(1)}, bf16[1024,512]{1,0:T(8,128)(2,1)S(1)}, bf16[512,256]{1,0:T(8,128)(2,1)S(1)}) custom-call(s32[1,2,8,8]{3,2,1,0:T(8,128)} %refs_0_.7, f32[1,2,64,1024]{3,2,1,0:T(8,128)} %refs_0_.6, f32[1,2,1024,512]{3,2,1,0:T(8,128)} %refs_1_.3, f32[1,2,512,128]{3,2,1,0:T(8,128)} %refs_4_.1), custom_call_target="tpu_custom_call" | custom-call | flops 536870912 | bytes 5243392 | tf_op jit(solution)/shard_map/pallas_call | solution.py:67
  6.9 1.6 %collective-permute-start.2 = (f32[128,512]{1,0:T(8,128)S(1)}, f32[128,512]{1,0:T(8,128)S(1)}, u32[]{:S(2)}, u32[]{:S(2)}) collective-permute-start(f32[128,512]{1,0:T(8,128)S(1)} %get-tuple-element.50.refs_2_), channel_id=1, source_target_pairs={{0,2},{2,4},{4,6},{6,7},{7,5},{5,3},{3,1},{1,0},{8,10},{10,12},{12... | collective-permute-start | bytes 786440 | tf_op jit(solution)/shard_map/ppermute | solution.py:383
  8.9 7.2 %collective-permute-done.1.refs_3_.refs_1_ = f32[2,128,512]{2,1,0:T(8,128)S(1)} collective-permute-done((f32[2,128,512]{2,1,0:T(8,128)S(1)}, f32[2,128,512]{2,1,0:T(8,128)S(1)}, u32[]{:S(2)}, u32[]{:S(2)}) %collective-permute-start.1) | collective-permute-done | bytes 524320 | tf_op jit(solution)/shard_map/ppermute | solution.py:363
  16.1 1.5 %shard_map.52.refs_7_ = f32[128,512]{1,0:T(8,128)S(1)} custom-call(s32[1,2,8,8]{3,2,1,0:T(8,128)} %refs_0_.7, f32[2,128,512]{2,1,0:T(8,128)S(1)} %collective-permute-done.1.refs_3_.refs_1_, bf16[1024,512]{1,0:T(8,128)(2,1)S(1)} %get-tuple-element.38.refs_0_.refs_2_, bf16[1024,512]{1,0:T(8,128)(2,1)S(1)} %get-tuple-element.39.refs_1_.refs_3_), custom_call_target="tpu_custom_call" | custom-call | flops 536870912 | bytes 2621952 | tf_op jit(solution)/shard_map/pallas_call | solution.py:67
  17.6 1.8 %collective-permute-start.6 = (f32[128,512]{1,0:T(8,128)S(1)}, f32[128,512]{1,0:T(8,128)S(1)}, u32[]{:S(2)}, u32[]{:S(2)}) collective-permute-start(f32[128,512]{1,0:T(8,128)S(1)} %shard_map.52.refs_7_), channel_id=1, source_target_pairs={{0,2},{2,4},{4,6},{6,7},{7,5},{5,3},{3,1},{1,0},{8,10},{10,12},{12... | collective-permute-start | bytes 786440 | tf_op jit(solution)/shard_map/ppermute | solution.py:383
  19.7 1.8 %collective-permute-start.4 = (f32[128,512]{1,0:T(8,128)S(1)}, f32[128,512]{1,0:T(8,128)S(1)}, u32[]{:S(2)}, u32[]{:S(2)}) collective-permute-start(f32[128,512]{1,0:T(8,128)S(1)} %collective-permute-done.2.refs_3_), channel_id=1, source_target_pairs={{0,2},{2,4},{4,6},{6,7},{7,5},{5,3},{3,1},{1,0},{8,10},{10,12},{12... | collective-permute-start | bytes 786440 | tf_op jit(solution)/shard_map/ppermute | solution.py:383
  21.5 1.2 %shard_map.47 = (f32[1024,128]{1,0:T(8,128)S(1)}, f32[512,512]{1,0:T(8,128)S(1)}, f32[512,128]{1,0:T(8,128)S(1)}) custom-call(bf16[1024,512]{1,0:T(8,128)(2,1)S(1)} %get-tuple-element.38.refs_0_.refs_2_, bf16[1024,512]{1,0:T(8,128)(2,1)S(1)} %get-tuple-element.39.refs_1_.refs_3_, bf16[512,256]{1,0:T(8,128)(2,1)S(1)} %get-tuple-element.40.refs_2_.refs_0_, ...), custom_call_target="tpu_custom_call" | custom-call | flops 536870912 | bytes 7077888 | tf_op jit(solution)/shard_map/pallas_call | solution.py:67
  22.8 1.6 %collective-permute-start = (f32[512,512]{1,0:T(8,128)S(1)}, f32[512,512]{1,0:T(8,128)S(1)}, u32[]{:S(2)}, u32[]{:S(2)}) collective-permute-start(f32[512,512]{1,0:T(8,128)S(1)} %get-tuple-element.42), channel_id=1, source_target_pairs={{0,8},{8,0},{1,9},{9,1},{2,10},{10,2},{3,11},{11,3},{4,12},{12,4},... | collective-permute-start | bytes 3145736 | tf_op jit(solution)/shard_map/ppermute | solution.py:411
  24.8 2.1 %collective-permute-done.6.refs_8_ = f32[128,512]{1,0:T(8,128)S(1)} collective-permute-done((f32[128,512]{1,0:T(8,128)S(1)}, f32[128,512]{1,0:T(8,128)S(1)}, u32[]{:S(2)}, u32[]{:S(2)}) %collective-permute-start.6) | collective-permute-done | bytes 262176 | tf_op jit(solution)/shard_map/ppermute | solution.py:383
  26.9 1.8 %collective-permute-start.8 = (f32[128,512]{1,0:T(8,128)S(1)}, f32[128,512]{1,0:T(8,128)S(1)}, u32[]{:S(2)}, u32[]{:S(2)}) collective-permute-start(f32[128,512]{1,0:T(8,128)S(1)} %collective-permute-done.6.refs_8_), channel_id=1, source_target_pairs={{0,2},{2,4},{4,6},{6,7},{7,5},{5,3},{3,1},{1,0},{8,10},{10,12},{12... | collective-permute-start | bytes 786440 | tf_op jit(solution)/shard_map/ppermute | solution.py:383
  28.9 3.6 %collective-permute-done.4.refs_5_ = f32[128,512]{1,0:T(8,128)S(1)} collective-permute-done((f32[128,512]{1,0:T(8,128)S(1)}, f32[128,512]{1,0:T(8,128)S(1)}, u32[]{:S(2)}, u32[]{:S(2)}) %collective-permute-start.4) | collective-permute-done | bytes 262176 | tf_op jit(solution)/shard_map/ppermute | solution.py:383
  32.5 1.8 %collective-permute-start.11 = (f32[128,512]{1,0:T(8,128)S(1)}, f32[128,512]{1,0:T(8,128)S(1)}, u32[]{:S(2)}, u32[]{:S(2)}) collective-permute-start(f32[128,512]{1,0:T(8,128)S(1)} %collective-permute-done.4.refs_5_), channel_id=1, source_target_pairs={{0,2},{2,4},{4,6},{6,7},{7,5},{5,3},{3,1},{1,0},{8,10},{10,12},{12... | collective-permute-start | bytes 786440 | tf_op jit(solution)/shard_map/ppermute | solution.py:383
  34.5 3.6 %collective-permute-done.8.refs_10_ = f32[128,512]{1,0:T(8,128)S(1)} collective-permute-done((f32[128,512]{1,0:T(8,128)S(1)}, f32[128,512]{1,0:T(8,128)S(1)}, u32[]{:S(2)}, u32[]{:S(2)}) %collective-permute-start.8) | collective-permute-done | bytes 262176 | tf_op jit(solution)/shard_map/ppermute | solution.py:383
  38.1 1.8 %collective-permute-start.13 = (f32[128,512]{1,0:T(8,128)S(1)}, f32[128,512]{1,0:T(8,128)S(1)}, u32[]{:S(2)}, u32[]{:S(2)}) collective-permute-start(f32[128,512]{1,0:T(8,128)S(1)} %collective-permute-done.8.refs_10_), channel_id=1, source_target_pairs={{0,2},{2,4},{4,6},{6,7},{7,5},{5,3},{3,1},{1,0},{8,10},{10,12},{12... | collective-permute-start | bytes 786440 | tf_op jit(solution)/shard_map/ppermute | solution.py:383
  40.9 2.8 %collective-permute-done.11.refs_2_ = f32[128,512]{1,0:T(8,128)S(1)} collective-permute-done((f32[128,512]{1,0:T(8,128)S(1)}, f32[128,512]{1,0:T(8,128)S(1)}, u32[]{:S(2)}, u32[]{:S(2)}) %collective-permute-start.11) | collective-permute-done | bytes 262176 | tf_op jit(solution)/shard_map/ppermute | solution.py:383
  43.7 1.7 %collective-permute-start.14 = (f32[128,512]{1,0:T(8,128)S(1)}, f32[128,512]{1,0:T(8,128)S(1)}, u32[]{:S(2)}, u32[]{:S(2)}) collective-permute-start(f32[128,512]{1,0:T(8,128)S(1)} %collective-permute-done.9.refs_11_), channel_id=1, source_target_pairs={{2,0},{4,2},{6,4},{7,6},{5,7},{3,5},{1,3},{0,1},{10,8},{12,10},{14... | collective-permute-start | bytes 786440 | tf_op jit(solution)/shard_map/ppermute | solution.py:384
  45.8 3.2 %collective-permute-done.13.refs_4_ = f32[128,512]{1,0:T(8,128)S(1)} collective-permute-done((f32[128,512]{1,0:T(8,128)S(1)}, f32[128,512]{1,0:T(8,128)S(1)}, u32[]{:S(2)}, u32[]{:S(2)}) %collective-permute-start.13) | collective-permute-done | bytes 262176 | tf_op jit(solution)/shard_map/ppermute | solution.py:383
  49.0 1.5 %collective-permute-start.17 = (f32[64,512]{1,0:T(8,128)S(1)}, f32[64,512]{1,0:T(8,128)S(1)}, u32[]{:S(2)}, u32[]{:S(2)}) collective-permute-start(f32[64,512]{1,0:T(8,128)S(1)} %slice.17), channel_id=1, source_target_pairs={{2,0},{4,2},{6,4},{7,6},{5,7},{3,5},{1,3},{0,1},{10,8},{12,10},{14... | collective-permute-start | bytes 393224 | tf_op jit(solution)/shard_map/ppermute | solution.py:397
  50.5 1.0 %collective-permute-done.14.refs_5_ = f32[128,512]{1,0:T(8,128)S(1)} collective-permute-done((f32[128,512]{1,0:T(8,128)S(1)}, f32[128,512]{1,0:T(8,128)S(1)}, u32[]{:S(2)}, u32[]{:S(2)}) %collective-permute-start.14) | collective-permute-done | bytes 262176 | tf_op jit(solution)/shard_map/ppermute | solution.py:384
  51.5 2.4 %collective-permute-start.18 = (f32[64,512]{1,0:T(8,128)S(1)}, f32[64,512]{1,0:T(8,128)S(1)}, u32[]{:S(2)}, u32[]{:S(2)}) collective-permute-start(f32[64,512]{1,0:T(8,128)S(1)} %slice.18), channel_id=1, source_target_pairs={{0,2},{2,4},{4,6},{6,7},{7,5},{5,3},{3,1},{1,0},{8,10},{10,12},{12... | collective-permute-start | bytes 393224 | tf_op jit(solution)/shard_map/ppermute | solution.py:396
  54.6 2.0 %collective-permute-start.21 = (f32[640,128]{1,0:T(8,128)S(1)}, f32[640,128]{1,0:T(8,128)S(1)}, u32[]{:S(2)}, u32[]{:S(2)}) collective-permute-start(f32[640,128]{1,0:T(8,128)S(1)} %add.9.refs_4_), channel_id=1, source_target_pairs={{0,8},{8,0},{1,9},{9,1},{2,10},{10,2},{3,11},{11,3},{4,12},{12,4},... | collective-permute-start | bytes 983048 | tf_op jit(solution)/shard_map/ppermute | solution.py:437
  56.8 2.2 %collective-permute-done.19.refs_5_ = f32[64,512]{1,0:T(8,128)S(1)} collective-permute-done((f32[64,512]{1,0:T(8,128)S(1)}, f32[64,512]{1,0:T(8,128)S(1)}, u32[]{:S(2)}, u32[]{:S(2)}) %collective-permute-start.19) | collective-permute-done | bytes 131104 | tf_op jit(solution)/shard_map/ppermute | solution.py:397
  59.4 1.6 %collective-permute-start.22 = (f32[256,128]{1,0:T(8,128)S(1)}, f32[256,128]{1,0:T(8,128)S(1)}, u32[]{:S(2)}, u32[]{:S(2)}) collective-permute-start(f32[256,128]{1,0:T(8,128)S(1)} %add.10.refs_5_), channel_id=1, source_target_pairs={{0,8},{8,0},{1,9},{9,1},{2,10},{10,2},{3,11},{11,3},{4,12},{12,4},... | collective-permute-start | bytes 393224 | tf_op jit(solution)/shard_map/ppermute | solution.py:437
  61.0 3.4 %shard_map.49 = (bf16[512,512]{1,0:T(8,128)(2,1)S(1)}, bf16[512,512]{1,0:T(8,128)(2,1)S(1)}, bf16[512,512]{1,0:T(8,128)(2,1)S(1)}, bf16[512,512]{1,0:T(8,128)(2,1)S(1)}) custom-call(f32[1,2,1024,512]{3,2,1,0:T(8,128)} %refs_1_.3), custom_call_target="tpu_custom_call" | custom-call | flops 1610612736 | bytes 4194304 | tf_op jit(solution)/shard_map/pallas_call | solution.py:67
  66.0 2.0 %collective-permute-done.22.refs_8_ = f32[256,128]{1,0:T(8,128)S(1)} collective-permute-done((f32[256,128]{1,0:T(8,128)S(1)}, f32[256,128]{1,0:T(8,128)S(1)}, u32[]{:S(2)}, u32[]{:S(2)}) %collective-permute-start.22) | collective-permute-done | bytes 131104 | tf_op jit(solution)/shard_map/ppermute | solution.py:437
  68.0 1.2 %collective-permute-done.23.refs_9_ = f32[128,128]{1,0:T(8,128)S(1)} collective-permute-done((f32[128,128]{1,0:T(8,128)S(1)}, f32[128,128]{1,0:T(8,128)S(1)}, u32[]{:S(2)}, u32[]{:S(2)}) %collective-permute-start.23) | collective-permute-done | bytes 65568 | tf_op jit(solution)/shard_map/ppermute | solution.py:437
  70.0 1.8 %collective-permute-start.25 = (f32[512,128]{1,0:T(8,128)S(1)}, f32[512,128]{1,0:T(8,128)S(1)}, u32[]{:S(2)}, u32[]{:S(2)}) collective-permute-start(f32[512,128]{1,0:T(8,128)S(1)} %shard_map.56.refs_1_), channel_id=1, source_target_pairs={{0,8},{8,0},{1,9},{9,1},{2,10},{10,2},{3,11},{11,3},{4,12},{12,4},... | collective-permute-start | bytes 786440 | tf_op jit(solution)/shard_map/ppermute | solution.py:448
  71.8 6.3 %collective-permute-done.25.refs_1_ = f32[512,128]{1,0:T(8,128)S(1)} collective-permute-done((f32[512,128]{1,0:T(8,128)S(1)}, f32[512,128]{1,0:T(8,128)S(1)}, u32[]{:S(2)}, u32[]{:S(2)}) %collective-permute-start.25) | collective-permute-done | bytes 262176 | tf_op jit(solution)/shard_map/ppermute | solution.py:448
  79.0 1.1 %shard_map.57 = (f32[512,128]{1,0:T(8,128)S(1)}, f32[1,2,512,128]{3,2,1,0:T(8,128)}) custom-call(f32[512,128]{1,0:T(8,128)S(1)} %shard_map.48.refs_0_, f32[512,128]{1,0:T(8,128)S(1)} %shard_map.56.refs_1_, f32[512,128]{1,0:T(8,128)S(1)} %collective-permute-done.24.refs_2_, bf16[512,640]{1,0:T(8,128)(2,1)S(1)} %get-tuple-element.57.refs_3_, ...), custom_call_target="tpu_custom_call" | custom-call | flops 536870912 | bytes 2883584 | tf_op jit(solution)/shard_map/pallas_call | solution.py:67
  80.1 1.5 %shard_map.58 = f32[1,2,512,128]{3,2,1,0:T(8,128)} custom-call(f32[512,128]{1,0:T(8,128)S(1)} %get-tuple-element.63.refs_0_, f32[512,128]{1,0:T(8,128)S(1)} %collective-permute-done.25.refs_1_, f32[512,128]{1,0:T(8,128)S(1)} %collective-permute-done.26.refs_2_, bf16[512,640]{1,0:T(8,128)(2,1)S(1)} %get-tuple-element.64.refs_3_, ...), custom_call_target="tpu_custom_call", output_to_operand_aliasing={{}: (9, {})} | custom-call | flops 536870912 | bytes 3407872 | tf_op jit(solution)/shard_map/pallas_call | solution.py:67
  (42 shorter events, 7.5 us)
Async XLA Ops:
  1.1 15.0 %collective-permute-start.1 = (f32[2,128,512]{2,1,0:T(8,128)S(1)}, f32[2,128,512]{2,1,0:T(8,128)S(1)}, u32[]{:S(2)}, u32[]{:S(2)}) collective-permute-start(f32[2,128,512]{2,1,0:T(8,128)S(1)} %shard_map.50), channel_id=1, source_target_pairs={{0,8},{8,0},{1,9},{9,1},{2,10},{10,2},{3,11},{11,3},{4,12},{12,4},... | collective-permute-start | bytes 1572872 | tf_op jit(solution)/shard_map/ppermute | solution.py:363
  6.9 12.8 %collective-permute-start.2 = (f32[128,512]{1,0:T(8,128)S(1)}, f32[128,512]{1,0:T(8,128)S(1)}, u32[]{:S(2)}, u32[]{:S(2)}) collective-permute-start(f32[128,512]{1,0:T(8,128)S(1)} %get-tuple-element.50.refs_2_), channel_id=1, source_target_pairs={{0,2},{2,4},{4,6},{6,7},{7,5},{5,3},{3,1},{1,0},{8,10},{10,12},{12... | collective-permute-start | bytes 786440 | tf_op jit(solution)/shard_map/ppermute | solution.py:383
  8.5 15.9 %collective-permute-start.3 = (f32[128,512]{1,0:T(8,128)S(1)}, f32[128,512]{1,0:T(8,128)S(1)}, u32[]{:S(2)}, u32[]{:S(2)}) collective-permute-start(f32[128,512]{1,0:T(8,128)S(1)} %get-tuple-element.50.refs_2_), channel_id=1, source_target_pairs={{2,0},{4,2},{6,4},{7,6},{5,7},{3,5},{1,3},{0,1},{10,8},{12,10},{14... | collective-permute-start | bytes 786440 | tf_op jit(solution)/shard_map/ppermute | solution.py:384
  17.6 9.2 %collective-permute-start.6 = (f32[128,512]{1,0:T(8,128)S(1)}, f32[128,512]{1,0:T(8,128)S(1)}, u32[]{:S(2)}, u32[]{:S(2)}) collective-permute-start(f32[128,512]{1,0:T(8,128)S(1)} %shard_map.52.refs_7_), channel_id=1, source_target_pairs={{0,2},{2,4},{4,6},{6,7},{7,5},{5,3},{3,1},{1,0},{8,10},{10,12},{12... | collective-permute-start | bytes 786440 | tf_op jit(solution)/shard_map/ppermute | solution.py:383
  19.5 9.2 %collective-permute-start.7 = (f32[128,512]{1,0:T(8,128)S(1)}, f32[128,512]{1,0:T(8,128)S(1)}, u32[]{:S(2)}, u32[]{:S(2)}) collective-permute-start(f32[128,512]{1,0:T(8,128)S(1)} %shard_map.52.refs_7_), channel_id=1, source_target_pairs={{2,0},{4,2},{6,4},{7,6},{5,7},{3,5},{1,3},{0,1},{10,8},{12,10},{14... | collective-permute-start | bytes 786440 | tf_op jit(solution)/shard_map/ppermute | solution.py:384
  19.7 12.8 %collective-permute-start.4 = (f32[128,512]{1,0:T(8,128)S(1)}, f32[128,512]{1,0:T(8,128)S(1)}, u32[]{:S(2)}, u32[]{:S(2)}) collective-permute-start(f32[128,512]{1,0:T(8,128)S(1)} %collective-permute-done.2.refs_3_), channel_id=1, source_target_pairs={{0,2},{2,4},{4,6},{6,7},{7,5},{5,3},{3,1},{1,0},{8,10},{10,12},{12... | collective-permute-start | bytes 786440 | tf_op jit(solution)/shard_map/ppermute | solution.py:383
  22.8 42.2 %collective-permute-start = (f32[512,512]{1,0:T(8,128)S(1)}, f32[512,512]{1,0:T(8,128)S(1)}, u32[]{:S(2)}, u32[]{:S(2)}) collective-permute-start(f32[512,512]{1,0:T(8,128)S(1)} %get-tuple-element.42), channel_id=1, source_target_pairs={{0,8},{8,0},{1,9},{9,1},{2,10},{10,2},{3,11},{11,3},{4,12},{12,4},... | collective-permute-start | bytes 3145736 | tf_op jit(solution)/shard_map/ppermute | solution.py:411
  24.3 9.9 %collective-permute-start.5 = (f32[128,512]{1,0:T(8,128)S(1)}, f32[128,512]{1,0:T(8,128)S(1)}, u32[]{:S(2)}, u32[]{:S(2)}) collective-permute-start(f32[128,512]{1,0:T(8,128)S(1)} %collective-permute-done.3.refs_4_), channel_id=1, source_target_pairs={{2,0},{4,2},{6,4},{7,6},{5,7},{3,5},{1,3},{0,1},{10,8},{12,10},{14... | collective-permute-start | bytes 786440 | tf_op jit(solution)/shard_map/ppermute | solution.py:384
  26.9 11.2 %collective-permute-start.8 = (f32[128,512]{1,0:T(8,128)S(1)}, f32[128,512]{1,0:T(8,128)S(1)}, u32[]{:S(2)}, u32[]{:S(2)}) collective-permute-start(f32[128,512]{1,0:T(8,128)S(1)} %collective-permute-done.6.refs_8_), channel_id=1, source_target_pairs={{0,2},{2,4},{4,6},{6,7},{7,5},{5,3},{3,1},{1,0},{8,10},{10,12},{12... | collective-permute-start | bytes 786440 | tf_op jit(solution)/shard_map/ppermute | solution.py:383
  28.6 11.2 %collective-permute-start.9 = (f32[128,512]{1,0:T(8,128)S(1)}, f32[128,512]{1,0:T(8,128)S(1)}, u32[]{:S(2)}, u32[]{:S(2)}) collective-permute-start(f32[128,512]{1,0:T(8,128)S(1)} %collective-permute-done.7.refs_9_), channel_id=1, source_target_pairs={{2,0},{4,2},{6,4},{7,6},{5,7},{3,5},{1,3},{0,1},{10,8},{12,10},{14... | collective-permute-start | bytes 786440 | tf_op jit(solution)/shard_map/ppermute | solution.py:384
  32.5 11.2 %collective-permute-start.11 = (f32[128,512]{1,0:T(8,128)S(1)}, f32[128,512]{1,0:T(8,128)S(1)}, u32[]{:S(2)}, u32[]{:S(2)}) collective-permute-start(f32[128,512]{1,0:T(8,128)S(1)} %collective-permute-done.4.refs_5_), channel_id=1, source_target_pairs={{0,2},{2,4},{4,6},{6,7},{7,5},{5,3},{3,1},{1,0},{8,10},{10,12},{12... | collective-permute-start | bytes 786440 | tf_op jit(solution)/shard_map/ppermute | solution.py:383
  34.3 11.2 %collective-permute-start.12 = (f32[128,512]{1,0:T(8,128)S(1)}, f32[128,512]{1,0:T(8,128)S(1)}, u32[]{:S(2)}, u32[]{:S(2)}) collective-permute-start(f32[128,512]{1,0:T(8,128)S(1)} %collective-permute-done.5.refs_6_), channel_id=1, source_target_pairs={{2,0},{4,2},{6,4},{7,6},{5,7},{3,5},{1,3},{0,1},{10,8},{12,10},{14... | collective-permute-start | bytes 786440 | tf_op jit(solution)/shard_map/ppermute | solution.py:384
  38.1 10.9 %collective-permute-start.13 = (f32[128,512]{1,0:T(8,128)S(1)}, f32[128,512]{1,0:T(8,128)S(1)}, u32[]{:S(2)}, u32[]{:S(2)}) collective-permute-start(f32[128,512]{1,0:T(8,128)S(1)} %collective-permute-done.8.refs_10_), channel_id=1, source_target_pairs={{0,2},{2,4},{4,6},{6,7},{7,5},{5,3},{3,1},{1,0},{8,10},{10,12},{12... | collective-permute-start | bytes 786440 | tf_op jit(solution)/shard_map/ppermute | solution.py:383
  40.8 13.6 %collective-permute-start.10 = (f32[640,128]{1,0:T(8,128)S(1)}, f32[640,128]{1,0:T(8,128)S(1)}, u32[]{:S(2)}, u32[]{:S(2)}) collective-permute-start(f32[640,128]{1,0:T(8,128)S(1)} %get-tuple-element.52), channel_id=1, source_target_pairs={{0,16},{16,0},{1,17},{17,1},{2,18},{18,2},{3,19},{19,3},{4,20},{20... | collective-permute-start | bytes 983048 | tf_op jit(solution)/shard_map/ppermute | solution.py:435
  43.7 7.8 %collective-permute-start.14 = (f32[128,512]{1,0:T(8,128)S(1)}, f32[128,512]{1,0:T(8,128)S(1)}, u32[]{:S(2)}, u32[]{:S(2)}) collective-permute-start(f32[128,512]{1,0:T(8,128)S(1)} %collective-permute-done.9.refs_11_), channel_id=1, source_target_pairs={{2,0},{4,2},{6,4},{7,6},{5,7},{3,5},{1,3},{0,1},{10,8},{12,10},{14... | collective-permute-start | bytes 786440 | tf_op jit(solution)/shard_map/ppermute | solution.py:384
  45.5 8.4 %collective-permute-start.16 = (f32[64,512]{1,0:T(8,128)S(1)}, f32[64,512]{1,0:T(8,128)S(1)}, u32[]{:S(2)}, u32[]{:S(2)}) collective-permute-start(f32[64,512]{1,0:T(8,128)S(1)} %slice.16), channel_id=1, source_target_pairs={{0,2},{2,4},{4,6},{6,7},{7,5},{5,3},{3,1},{1,0},{8,10},{10,12},{12... | collective-permute-start | bytes 393224 | tf_op jit(solution)/shard_map/ppermute | solution.py:396
  49.0 5.6 %collective-permute-start.17 = (f32[64,512]{1,0:T(8,128)S(1)}, f32[64,512]{1,0:T(8,128)S(1)}, u32[]{:S(2)}, u32[]{:S(2)}) collective-permute-start(f32[64,512]{1,0:T(8,128)S(1)} %slice.17), channel_id=1, source_target_pairs={{2,0},{4,2},{6,4},{7,6},{5,7},{3,5},{1,3},{0,1},{10,8},{12,10},{14... | collective-permute-start | bytes 393224 | tf_op jit(solution)/shard_map/ppermute | solution.py:397
  51.5 5.2 %collective-permute-start.18 = (f32[64,512]{1,0:T(8,128)S(1)}, f32[64,512]{1,0:T(8,128)S(1)}, u32[]{:S(2)}, u32[]{:S(2)}) collective-permute-start(f32[64,512]{1,0:T(8,128)S(1)} %slice.18), channel_id=1, source_target_pairs={{0,2},{2,4},{4,6},{6,7},{7,5},{5,3},{3,1},{1,0},{8,10},{10,12},{12... | collective-permute-start | bytes 393224 | tf_op jit(solution)/shard_map/ppermute | solution.py:396
  53.9 5.0 %collective-permute-start.19 = (f32[64,512]{1,0:T(8,128)S(1)}, f32[64,512]{1,0:T(8,128)S(1)}, u32[]{:S(2)}, u32[]{:S(2)}) collective-permute-start(f32[64,512]{1,0:T(8,128)S(1)} %slice.19), channel_id=1, source_target_pairs={{2,0},{4,2},{6,4},{7,6},{5,7},{3,5},{1,3},{0,1},{10,8},{12,10},{14... | collective-permute-start | bytes 393224 | tf_op jit(solution)/shard_map/ppermute | solution.py:397
  54.5 4.9 %collective-permute-start.15 = (f32[256,128]{1,0:T(8,128)S(1)}, f32[256,128]{1,0:T(8,128)S(1)}, u32[]{:S(2)}, u32[]{:S(2)}) collective-permute-start(f32[256,128]{1,0:T(8,128)S(1)} %get-tuple-element.54), channel_id=1, source_target_pairs={{0,16},{16,0},{1,17},{17,1},{2,18},{18,2},{3,19},{19,3},{4,20},{20... | collective-permute-start | bytes 393224 | tf_op jit(solution)/shard_map/ppermute | solution.py:435
  54.6 14.6 %collective-permute-start.21 = (f32[640,128]{1,0:T(8,128)S(1)}, f32[640,128]{1,0:T(8,128)S(1)}, u32[]{:S(2)}, u32[]{:S(2)}) collective-permute-start(f32[640,128]{1,0:T(8,128)S(1)} %add.9.refs_4_), channel_id=1, source_target_pairs={{0,8},{8,0},{1,9},{9,1},{2,10},{10,2},{3,11},{11,3},{4,12},{12,4},... | collective-permute-start | bytes 983048 | tf_op jit(solution)/shard_map/ppermute | solution.py:437
  59.3 5.1 %collective-permute-start.20 = (f32[128,128]{1,0:T(8,128)S(1)}, f32[128,128]{1,0:T(8,128)S(1)}, u32[]{:S(2)}, u32[]{:S(2)}) collective-permute-start(f32[128,128]{1,0:T(8,128)S(1)} %get-tuple-element.56), channel_id=1, source_target_pairs={{0,16},{16,0},{1,17},{17,1},{2,18},{18,2},{3,19},{19,3},{4,20},{20... | collective-permute-start | bytes 196616 | tf_op jit(solution)/shard_map/ppermute | solution.py:435
  59.4 8.7 %collective-permute-start.22 = (f32[256,128]{1,0:T(8,128)S(1)}, f32[256,128]{1,0:T(8,128)S(1)}, u32[]{:S(2)}, u32[]{:S(2)}) collective-permute-start(f32[256,128]{1,0:T(8,128)S(1)} %add.10.refs_5_), channel_id=1, source_target_pairs={{0,8},{8,0},{1,9},{9,1},{2,10},{10,2},{3,11},{11,3},{4,12},{12,4},... | collective-permute-start | bytes 393224 | tf_op jit(solution)/shard_map/ppermute | solution.py:437
  64.4 4.8 %collective-permute-start.23 = (f32[128,128]{1,0:T(8,128)S(1)}, f32[128,128]{1,0:T(8,128)S(1)}, u32[]{:S(2)}, u32[]{:S(2)}) collective-permute-start(f32[128,128]{1,0:T(8,128)S(1)} %add.11.refs_6_), channel_id=1, source_target_pairs={{0,8},{8,0},{1,9},{9,1},{2,10},{10,2},{3,11},{11,3},{4,12},{12,4},... | collective-permute-start | bytes 196616 | tf_op jit(solution)/shard_map/ppermute | solution.py:437
  70.0 8.1 %collective-permute-start.25 = (f32[512,128]{1,0:T(8,128)S(1)}, f32[512,128]{1,0:T(8,128)S(1)}, u32[]{:S(2)}, u32[]{:S(2)}) collective-permute-start(f32[512,128]{1,0:T(8,128)S(1)} %shard_map.56.refs_1_), channel_id=1, source_target_pairs={{0,8},{8,0},{1,9},{9,1},{2,10},{10,2},{3,11},{11,3},{4,12},{12,4},... | collective-permute-start | bytes 786440 | tf_op jit(solution)/shard_map/ppermute | solution.py:448
  71.8 7.2 %collective-permute-start.24 = (f32[512,128]{1,0:T(8,128)S(1)}, f32[512,128]{1,0:T(8,128)S(1)}, u32[]{:S(2)}, u32[]{:S(2)}) collective-permute-start(f32[512,128]{1,0:T(8,128)S(1)} %shard_map.56.refs_1_), channel_id=1, source_target_pairs={{0,16},{16,0},{1,17},{17,1},{2,18},{18,2},{3,19},{19,3},{4,20},{20... | collective-permute-start | bytes 786440 | tf_op jit(solution)/shard_map/ppermute | solution.py:449
  78.1 2.0 %collective-permute-start.26 = (f32[512,128]{1,0:T(8,128)S(1)}, f32[512,128]{1,0:T(8,128)S(1)}, u32[]{:S(2)}, u32[]{:S(2)}) collective-permute-start(f32[512,128]{1,0:T(8,128)S(1)} %collective-permute-done.25.refs_1_), channel_id=1, source_target_pairs={{0,16},{16,0},{1,17},{17,1},{2,18},{18,2},{3,19},{19,3},{4,20},{20... | collective-permute-start | bytes 786440 | tf_op jit(solution)/shard_map/ppermute | solution.py:450
